TPU v7x, 32 devices: a whole 2x2x4 slice. The times are simulated.
32 devices in a mesh: pipe: 8 (over y, x, core), tensor: 4 (over z).
Axes of the slice: x: 2, y: 2, z: 4, core: 2. Of those that a mesh axis runs over, the one named last changes fastest.
Arguments:
- fwd_inputs: bfloat16 [8, 576, 1536], P('pipe'), may hold values from -6 to 6
- bwd_inputs: bfloat16 [8, 576, 1536], P('pipe'), may hold values from -6 to 6
- bwd_cotangent: bfloat16 [8, 576, 1536], P('pipe'), may hold values from -6 to 6
- fwd_lengths: int32 [8, 8], P('pipe'), may hold values from 1 to 192, 576 in all within a row
- bwd_lengths: int32 [8, 8], P('pipe'), may hold values from 1 to 192, 576 in all within a row
- norm_gains: bfloat16 [2, 8, 1536], P(None, 'pipe'), may hold values from 0.25 to 1.75
- query_weight: bfloat16 [2, 8, 1536, 1536], P(None, 'pipe', None, 'tensor'), may hold values from -1 to 1
- key_weight: bfloat16 [2, 8, 1536, 1536], P(None, 'pipe', None, 'tensor'), may hold values from -1 to 1
- value_weight: bfloat16 [2, 8, 1536, 1536], P(None, 'pipe', None, 'tensor'), may hold values from -0.15625 to 0.15625
- out_weight: bfloat16 [2, 8, 1536, 1536], P(None, 'pipe', 'tensor'), may hold values from -0.15625 to 0.15625
Outputs:
- next_inputs: bfloat16 [8, 576, 1536], P('pipe', 'tensor')
- next_cotangent: bfloat16 [8, 576, 1536], P('pipe', 'tensor')
- out_weight_grad: float32 [8, 1536, 1536], P('pipe', 'tensor')
Inputs may be any that keep to these rules, and one draw needn't show every extreme that they name: `fwd_lengths`: each microbatch's mesh lengths sum to 576; the longest is exactly 192. `bwd_lengths`: each microbatch's mesh lengths sum to 576; the longest is exactly 192.
All inputs are finite; a program needn't handle non-finite values.
Results may differ from a plain program's by a relative error of at most 0.019.
Values may be sent and summed in bfloat16 or wider, within the bound.
A program may use at most 64 MiB of HBM per device.

v0:
```python
import jax
import jax.numpy as jnp
from jax import lax
from jax.sharding import PartitionSpec as P

HEAD_DIM = 128


def passed_along(value, axis, by):
    peers = lax.axis_size(axis)
    pairs = [(i, i + by) for i in range(peers) if 0 <= i + by < peers]
    return lax.ppermute(value, axis, pairs)


def from_partner(value, axis, distance):
    mask = 2**distance
    pairs = [(source, source ^ mask) for source in range(lax.axis_size(axis))]
    return lax.ppermute(value, axis, pairs)


def rms_norm(activation, gain_vec):
    widened = activation.astype(jnp.float32)
    mean_square = jnp.mean(widened * widened, axis=-1, keepdims=True)
    return (widened * lax.rsqrt(mean_square + 1e-05) * gain_vec.astype(jnp.float32)).astype(
        jnp.bfloat16
    )


def doc_mask(lengths, row_count):
    doc_ends = jnp.cumsum(lengths)
    position = jnp.arange(row_count, dtype=jnp.int32)
    segment = jnp.sum((position[:, None] >= doc_ends[None, :]).astype(jnp.int32), axis=1)
    return (segment[:, None] == segment[None, :]) & (position[None, :] <= position[:, None])


def head_block(normed, w_query, w_key, w_value, w_out, keep_mask):
    row_count = normed.shape[0]
    group_count = w_query.shape[1] // HEAD_DIM

    def project(weight):
        return (
            jnp.dot(normed, weight, preferred_element_type=jnp.float32)
            .astype(jnp.bfloat16)
            .reshape(row_count, group_count, HEAD_DIM)
        )

    queries = project(w_query)
    key_rows = project(w_key)
    value_rows = project(w_value)
    scores = jnp.einsum(
        "qgh,kgh->gqk", queries.astype(jnp.float32), key_rows.astype(jnp.float32)
    ) * HEAD_DIM ** (-0.5)
    scores = jnp.where(keep_mask[None], scores, -1e30)
    row_max = jnp.max(scores, axis=-1, keepdims=True)
    weights = jnp.where(keep_mask[None], jnp.exp(scores - row_max), 0.0)
    weights_bf = (weights / jnp.sum(weights, axis=-1, keepdims=True)).astype(jnp.bfloat16)
    attended = jnp.einsum(
        "gqk,kgh->qgh", weights_bf.astype(jnp.float32), value_rows.astype(jnp.float32)
    ).astype(jnp.bfloat16)
    attended = attended.reshape(row_count, group_count * HEAD_DIM)
    return (jnp.dot(attended, w_out, preferred_element_type=jnp.float32), attended)


def per_device(
    fwd_inputs,
    bwd_inputs,
    bwd_cotangent,
    fwd_lengths,
    bwd_lengths,
    norm_gains,
    query_weight,
    key_weight,
    value_weight,
    out_weight,
):
    row_count = fwd_inputs.shape[1]
    share_rows = row_count // lax.axis_size("tensor")
    row_start = lax.axis_index("tensor") * share_rows
    forward_in = fwd_inputs[0]
    forward_mask = doc_mask(fwd_lengths[0], row_count)
    forward_term, unused = head_block(
        rms_norm(forward_in, norm_gains[0, 0]),
        query_weight[0, 0],
        key_weight[0, 0],
        value_weight[0, 0],
        out_weight[0, 0],
        forward_mask,
    )
    backward_in = bwd_inputs[0]
    cotangent = bwd_cotangent[0]
    backward_mask = doc_mask(bwd_lengths[0], row_count)

    def branch(activation):
        return head_block(
            rms_norm(activation, norm_gains[1, 0]),
            query_weight[1, 0],
            key_weight[1, 0],
            value_weight[1, 0],
            out_weight[1, 0],
            backward_mask,
        )

    unused_out, pull_back, attended = jax.vjp(branch, backward_in, has_aux=True)
    (input_grad,) = pull_back(cotangent.astype(jnp.float32))
    weight_grad = lax.dot_general(
        attended, cotangent, (((0,), (0,)), ((), ())), preferred_element_type=jnp.float32
    )
    backward_term = input_grad.astype(jnp.float32)
    whole_forward, whole_backward = (
        lax.psum(forward_term.astype(jnp.bfloat16), "tensor").astype(jnp.float32),
        lax.psum(backward_term.astype(jnp.bfloat16), "tensor").astype(jnp.float32),
    )
    summed_forward = lax.dynamic_slice_in_dim(whole_forward, row_start, share_rows, 0)
    summed_backward = lax.dynamic_slice_in_dim(whole_backward, row_start, share_rows, 0)
    forward_rows = lax.dynamic_slice_in_dim(forward_in, row_start, share_rows, 0)
    cotangent_rows = lax.dynamic_slice_in_dim(cotangent, row_start, share_rows, 0)
    section_rows = (forward_rows.astype(jnp.float32) + summed_forward).astype(jnp.bfloat16)
    grad_rows = (cotangent_rows.astype(jnp.float32) + summed_backward).astype(jnp.bfloat16)
    moved_section, moved_grad = passed_along((section_rows, grad_rows), "pipe", 1)
    bit_total = lax.axis_size("pipe").bit_length() - 1
    bit_order = list(range(bit_total))
    mirrored = weight_grad
    for bit_index in bit_order:
        mirrored = from_partner(mirrored.astype(jnp.bfloat16), "pipe", bit_index).astype(
            mirrored.dtype
        )
    return (moved_section[None], moved_grad[None], mirrored[None])


def solution(mesh):
    placed = (
        P("pipe", None, None),
        P("pipe", None, None),
        P("pipe", None, None),
        P("pipe", None),
        P("pipe", None),
        P(None, "pipe", None),
        P(None, "pipe", None, "tensor"),
        P(None, "pipe", None, "tensor"),
        P(None, "pipe", None, "tensor"),
        P(None, "pipe", "tensor", None),
    )
    return jax.shard_map(
        per_device,
        mesh=mesh,
        in_specs=placed,
        out_specs=(P("pipe", "tensor", None), P("pipe", "tensor", None), P("pipe", "tensor", None)),
        check_vma=False,
    )
```

profile of v0, /device:TPU:4, one launch (start us, length us, event | category | flops | bytes accessed | tf_op | source)
XLA Modules:
  0.0 242.6 jit_solution(17265965038565359189)
XLA Ops:
  9.9 3.1 %convolution_convert_fusion.10 = bf16[576,384]{1,0:T(8,128)(2,1)S(1)} fusion(bf16[2,1,1536,384]{3,2,1,0:T(8,128)(2,1)} %param.16, bf16[1,576,1536]{2,1,0:T(8,128)(2,1)} %param.11, f32[1536]{0:T(1024)S(1)} %get-tuple-element.3, f32[576]{0:T(1024)S(1)} %fusion.80), kind=kOutput, calls=%fused_computation.75 | convolution fusion | flops 683237376 | bytes 3399936 | tf_op jit(solution)/shard_map/jvp()/dot_general | solution.py:42
  13.3 2.6 %convolution_convert_fusion.9 = bf16[576,384]{1,0:T(8,128)(2,1)S(1)} fusion(bf16[2,1,1536,384]{3,2,1,0:T(8,128)(2,1)} %param.17, bf16[1,576,1536]{2,1,0:T(8,128)(2,1)S(1)} %copy-done.1, f32[1536]{0:T(1024)S(1)} %get-tuple-element.3, f32[576]{0:T(1024)S(1)} %fusion.80), kind=kOutput, calls=%fused_computation.74 | convolution fusion | flops 683237376 | bytes 3399936 | tf_op jit(solution)/shard_map/jvp()/dot_general | solution.py:42
  17.4 2.1 fusion.96
  24.3 2.9 %fusion.43 = bf16[576,384]{1,0:T(8,128)(2,1)S(1)} fusion(bf16[1,576,1536]{2,1,0:T(8,128)(2,1)} %param.12, bf16[2,1,384,1536]{3,2,1,0:T(8,128)(2,1)} %param.19), kind=kOutput, calls=%fused_computation.67 | convolution fusion | flops 679698432 | bytes 3391488 | tf_op jit(solution)/shard_map/transpose(jvp())/dot_general | solution.py:61
  27.5 5.0 %convert_reduce_fusion = (f32[3,576]{1,0:T(4,128)S(1)}, pred[3,576,576]{1,2,0:T(32,128)(4,1)S(1)}, f32[3,576]{1,0:T(4,128)S(1)}, bf16[3,576,576]{1,2,0:T(8,128)(2,1)S(1)}) fusion(f32[3,576,576]{1,2,0:T(8,128)} %copy-done, f32[3,576]{1,0:T(4,128)S(1)} %get-tuple-element.15, pred[576,576]{0,1:T(8,128)(4,1)S(1)} %fusion.41, ...), kind=kOutput, calls=%fused_computation.10 | convolution fusion | flops 264753792 | bytes 8211456 | tf_op jit(solution)/shard_map/transpose(jvp(gqk,kgh->qgh))/dot_general | solution.py:57
  32.6 2.1 fusion.93
  36.4 2.1 fusion.52
  47.0 3.7 %convolution_convert_fusion.1 = bf16[576,1536]{1,0:T(8,128)(2,1)} fusion(bf16[576,384]{0,1:T(8,128)(2,1)S(1)} %bitcast.139, bf16[2,1,1536,384]{3,2,1,0:T(8,128)(2,1)} %param.17), kind=kOutput, calls=%fused_computation.36 | convolution fusion | flops 680361984 | bytes 3391488 | tf_op jit(solution)/shard_map/transpose(jvp())/dot_general | solution.py:42
  52.4 3.3 %fusion.19 = bf16[576,1536]{1,0:T(8,128)(2,1)S(1)} fusion(bf16[576,1536]{1,0:T(8,128)(2,1)} %convolution_convert_fusion.1, bf16[576,384]{0,1:T(8,128)(2,1)} %bitcast.138, bf16[2,1,1536,384]{3,2,1,0:T(8,128)(2,1)} %param.18), kind=kOutput, calls=%fused_computation.39 | convolution fusion | flops 681246720 | bytes 5210112 | tf_op jit(solution)/shard_map/transpose(jvp())/dot_general | solution.py:42
  55.8 2.6 %fusion.14 = (f32[576]{0:T(1024)S(1)}, bf16[576,1536]{1,0:T(8,128)(2,1)}) fusion(bf16[1,576,1536]{2,1,0:T(8,128)(2,1)S(1)} %copy-done.2, f32[1536]{0:T(1024)S(1)} %get-tuple-element.3, bf16[576,1536]{1,0:T(8,128)(2,1)S(1)} %fusion.19, bf16[576,384]{0,1:T(8,128)(2,1)S(1)} %bitcast.134, bf16[2,1,1536,384]{3,2,1,0:T(8,128)(2,1)S(1)} %copy-done.16), kind=kOutput, calls=%fused_computation.29 | convolution fusion | flops 685669824 | bytes 6990080 | tf_op jit(solution)/shard_map/transpose(jvp())/dot_general | solution.py:42
  59.7 2.0 copy.54
  63.0 2.0 copy.52
  65.0 5.8 %fusion.95 = (f32[3,576]{1,0:T(4,128)S(1)}, f32[3,576,576]{1,2,0:T(8,128)}) fusion(pred[576,576]{0,1:T(8,128)(4,1)} %fusion.42, bf16[576,3,128]{0,2,1:T(8,128)(2,1)S(1)} %bitcast.135, bf16[576,3,128]{0,2,1:T(8,128)(2,1)} %bitcast.136), kind=kOutput, calls=%fused_computation.131 | convolution fusion | flops 259781184 | bytes 5204736 | tf_op jit(solution)/shard_map/sub | solution.py:55
  70.8 4.2 %fusion.53 = bf16[576,3,128]{2,0,1:T(8,128)(2,1)} fusion(bf16[576,3,128]{0,2,1:T(8,128)(2,1)} %bitcast.137, f32[3,576,576]{1,2,0:T(8,128)} %get-tuple-element.14, f32[3,576]{1,0:T(4,128)S(1)} %get-tuple-element.13), kind=kOutput, calls=%fused_computation.83 | convolution fusion | flops 257015808 | bytes 4872960 | tf_op jit(solution)/shard_map/gqk,kgh->qgh/dot_general | solution.py:57
  76.2 3.7 %convolution_convert_fusion.3 = bf16[576,1536]{1,0:T(8,128)(2,1)} fusion(bf16[576,384]{0,1:T(8,128)(2,1)S(1)} %bitcast.140, bf16[2,1,384,1536]{3,2,1,0:T(8,128)(2,1)} %param.19), kind=kOutput, calls=%fused_computation.38 | convolution fusion | flops 680361984 | bytes 3391488 | tf_op jit(solution)/shard_map/dot_general | solution.py:61
  80.0 2.1 fusion.17
  83.4 2.6 %convolution_convert_fusion.4 = bf16[384,1536]{1,0:T(8,128)(2,1)S(1)} fusion(bf16[576,384]{0,1:T(8,128)(2,1)S(1)} %bitcast.141, bf16[1,576,1536]{2,1,0:T(8,128)(2,1)} %param.12), kind=kOutput, calls=%fused_computation.44 | convolution fusion | flops 680067072 | bytes 3391488 | tf_op jit(solution)/shard_map/dot_general | solution.py:105
  86.0 2.8 %collective-permute-done.2 = bf16[384,1536]{1,0:T(8,128)(2,1)S(1)} collective-permute-done((bf16[384,1536]{1,0:T(8,128)(2,1)S(1)}, bf16[384,1536]{1,0:T(8,128)(2,1)S(1)}, u32[]{:S(2)}, u32[]{:S(2)}) %collective-permute-start.2) | collective-permute-done | bytes 1179680 | tf_op jit(solution)/shard_map/ppermute | solution.py:18
  90.3 26.5 %collective-permute-done.3 = bf16[384,1536]{1,0:T(8,128)(2,1)S(1)} collective-permute-done((bf16[384,1536]{1,0:T(8,128)(2,1)S(1)}, bf16[384,1536]{1,0:T(8,128)(2,1)S(1)}, u32[]{:S(2)}, u32[]{:S(2)}) %collective-permute-start.3) | collective-permute-done | bytes 1179680 | tf_op jit(solution)/shard_map/ppermute | solution.py:18
  117.1 100.6 %all-reduce.3.cloned.1.call-done = (bf16[576,1536]{1,0:T(8,128)(2,1)}, bf16[576,1536]{1,0:T(8,128)(2,1)}) async-done(((bf16[576,1536]{1,0:T(8,128)(2,1)}, bf16[576,1536]{1,0:T(8,128)(2,1)}), (bf16[576,1536]{1,0:T(8,128)(2,1)}, bf16[576,1536]{1,0:T(8,128)(2,1)})) %all-reduce.3.cloned.1.call-update) | async-done | bytes 3538960 | tf_op jit(solution)/shard_map/psum | solution.py:110
  218.9 1.9 collective-permute-start.1
  222.1 3.5 %collective-permute-start = (bf16[144,1536]{1,0:T(8,128)(2,1)S(1)}, bf16[144,1536]{1,0:T(8,128)(2,1)S(1)}, u32[]{:S(2)}, u32[]{:S(2)}) collective-permute-start(bf16[144,1536]{1,0:T(8,128)(2,1)S(1)} %fusion.77), channel_id=1, source_target_pairs={{0,4},{4,8},{8,12},{12,16},{16,20},{20,24},{24,28},{1,5},{5,9},{9,... | collective-permute-start | bytes 1327112 | tf_op jit(solution)/shard_map/ppermute | solution.py:12
  227.3 2.1 collective-permute-done.1
  229.4 4.7 %collective-permute-done = bf16[144,1536]{1,0:T(8,128)(2,1)S(1)} collective-permute-done((bf16[144,1536]{1,0:T(8,128)(2,1)S(1)}, bf16[144,1536]{1,0:T(8,128)(2,1)S(1)}, u32[]{:S(2)}, u32[]{:S(2)}) %collective-permute-start) | collective-permute-done | bytes 442400 | tf_op jit(solution)/shard_map/ppermute | solution.py:12
  (87 shorter events, 34.1 us)
Async XLA Ops:
  7.2 210.5 %all-reduce.3.cloned.1.call-start = ((), (), s32[]{:S(2)}) async-start(), calls=%async_computation | async-start | bytes 7077888 | tf_op jit(solution)/shard_map/psum | solution.py:110
  9.9 3.3 %copy-start.1 = (bf16[1,576,1536]{2,1,0:T(8,128)(2,1)S(1)}, bf16[1,576,1536]{2,1,0:T(8,128)(2,1)}, u32[]{:S(2)}) copy-start(bf16[1,576,1536]{2,1,0:T(8,128)(2,1)} %param.11) | copy-start | bytes 5308420
  13.3 4.2 %copy-start.7 = (bf16[576,384]{0,1:T(8,128)(2,1)}, bf16[576,384]{0,1:T(8,128)(2,1)S(1)}, u32[]{:S(2)}) copy-start(bf16[576,384]{0,1:T(8,128)(2,1)S(1)} %copy.61) | copy-start | bytes 1327108
  13.3 3.6 %copy-start.17 = (s32[1,8]{1,0:T(1,128)S(1)}, s32[1,8]{1,0:T(1,128)}, u32[]{:S(2)}) copy-start(s32[1,8]{1,0:T(1,128)} %param.14) | copy-start | bytes 100
  19.6 2.3 copy-start
  19.6 3.3 %copy-start.13 = (bf16[2,1,1536,384]{3,2,1,0:T(8,128)(2,1)S(1)}, bf16[2,1,1536,384]{3,2,1,0:T(8,128)(2,1)}, u32[]{:S(2)}) copy-start(bf16[2,1,1536,384]{3,2,1,0:T(8,128)(2,1)} %param.18) | copy-start | bytes 7077892
  27.4 5.1 %copy-start.5 = (bf16[576,384]{0,1:T(8,128)(2,1)}, bf16[576,384]{0,1:T(8,128)(2,1)S(1)}, u32[]{:S(2)}) copy-start(bf16[576,384]{0,1:T(8,128)(2,1)S(1)} %copy.60) | copy-start | bytes 1327108
  27.5 5.1 %slice-start = ((s8[4423680]{0:T(1024)(128)(4,1)}), s8[4194304]{0:T(1024)(128)(4,1)S(1)}, s32[]{:S(2)}) async-start(s8[4423680]{0:T(1024)(128)(4,1)} %bitcast.124), calls=%async_computation.1 | async-start | bytes 8388608
  27.5 5.1 %slice-start.1 = ((s8[4423680]{0:T(1024)(128)(4,1)}), s8[229376]{0:T(1024)(128)(4,1)S(1)}, s32[]{:S(2)}) async-start(s8[4423680]{0:T(1024)(128)(4,1)} %bitcast.124), calls=%async_computation.2 | async-start | bytes 458752
  32.6 2.1 copy-start.9
  36.4 2.2 copy-start.4
  36.4 2.6 %copy-start.15 = (bf16[2,1,1536,384]{3,2,1,0:T(8,128)(2,1)S(1)}, bf16[2,1,1536,384]{3,2,1,0:T(8,128)(2,1)}, u32[]{:S(2)}) copy-start(bf16[2,1,1536,384]{3,2,1,0:T(8,128)(2,1)} %param.16) | copy-start | bytes 7077892
  47.0 3.7 %copy-start.6 = (bf16[576,384]{0,1:T(8,128)(2,1)S(1)}, bf16[576,384]{0,1:T(8,128)(2,1)}, u32[]{:S(2)}) copy-start(bf16[576,384]{0,1:T(8,128)(2,1)} %copy-done.5) | copy-start | bytes 1327108
  52.4 3.3 %copy-start.2 = (bf16[1,576,1536]{2,1,0:T(8,128)(2,1)S(1)}, bf16[1,576,1536]{2,1,0:T(8,128)(2,1)}, u32[]{:S(2)}) copy-start(bf16[1,576,1536]{2,1,0:T(8,128)(2,1)} %param.11) | copy-start | bytes 5308420
  52.4 3.3 %copy-start.11 = (bf16[576,3,128]{0,2,1:T(8,128)(2,1)S(1)}, bf16[576,3,128]{0,2,1:T(8,128)(2,1)}, u32[]{:S(2)}) copy-start(bf16[576,3,128]{0,2,1:T(8,128)(2,1)} %copy.74) | copy-start | bytes 1327108
  52.4 3.4 %copy-start.16 = (bf16[2,1,1536,384]{3,2,1,0:T(8,128)(2,1)S(1)}, bf16[2,1,1536,384]{3,2,1,0:T(8,128)(2,1)}, u32[]{:S(2)}) copy-start(bf16[2,1,1536,384]{3,2,1,0:T(8,128)(2,1)} %param.16) | copy-start | bytes 7077892
  55.8 5.9 %copy-start.18 = (s32[1,8]{1,0:T(1,128)S(1)}, s32[1,8]{1,0:T(1,128)}, u32[]{:S(2)}) copy-start(s32[1,8]{1,0:T(1,128)} %param.13) | copy-start | bytes 100
  76.2 3.8 %copy-start.3 = (bf16[1,576,1536]{2,1,0:T(8,128)(2,1)S(1)}, bf16[1,576,1536]{2,1,0:T(8,128)(2,1)}, u32[]{:S(2)}) copy-start(bf16[1,576,1536]{2,1,0:T(8,128)(2,1)} %param.11) | copy-start | bytes 5308420
  76.2 3.8 %copy-start.10 = (bf16[576,1536]{1,0:T(8,128)(2,1)S(1)}, bf16[576,1536]{1,0:T(8,128)(2,1)}, u32[]{:S(2)}) copy-start(bf16[576,1536]{1,0:T(8,128)(2,1)} %get-tuple-element.19) | copy-start | bytes 5308420
  85.9 2.9 %collective-permute-start.2 = (bf16[384,1536]{1,0:T(8,128)(2,1)S(1)}, bf16[384,1536]{1,0:T(8,128)(2,1)S(1)}, u32[]{:S(2)}, u32[]{:S(2)}) collective-permute-start(bf16[384,1536]{1,0:T(8,128)(2,1)S(1)} %convolution_convert_fusion.4), channel_id=1, source_target_pairs={{0,4},{4,0},{8,12},{12,8},{16,20},{20,16},{24,28},{28,24},{1,5},{5... | collective-permute-start | bytes 3538952 | tf_op jit(solution)/shard_map/ppermute | solution.py:18
  88.8 28.0 %collective-permute-start.3 = (bf16[384,1536]{1,0:T(8,128)(2,1)S(1)}, bf16[384,1536]{1,0:T(8,128)(2,1)S(1)}, u32[]{:S(2)}, u32[]{:S(2)}) collective-permute-start(bf16[384,1536]{1,0:T(8,128)(2,1)S(1)} %collective-permute-done.2), channel_id=1, source_target_pairs={{0,8},{4,12},{8,0},{12,4},{16,24},{20,28},{24,16},{28,20},{1,9},{5... | collective-permute-start | bytes 3538952 | tf_op jit(solution)/shard_map/ppermute | solution.py:18
  116.8 108.8 %collective-permute-start.4 = (bf16[384,1536]{1,0:T(8,128)(2,1)S(1)}, bf16[384,1536]{1,0:T(8,128)(2,1)S(1)}, u32[]{:S(2)}, u32[]{:S(2)}) collective-permute-start(bf16[384,1536]{1,0:T(8,128)(2,1)S(1)} %collective-permute-done.3), channel_id=1, source_target_pairs={{0,16},{4,20},{8,24},{12,28},{16,0},{20,4},{24,8},{28,12},{1,17},{... | collective-permute-start | bytes 3538952 | tf_op jit(solution)/shard_map/ppermute | solution.py:18
  218.9 10.5 %collective-permute-start.1 = (bf16[144,1536]{1,0:T(8,128)(2,1)S(1)}, bf16[144,1536]{1,0:T(8,128)(2,1)S(1)}, u32[]{:S(2)}, u32[]{:S(2)}) collective-permute-start(bf16[144,1536]{1,0:T(8,128)(2,1)S(1)} %fusion.76), channel_id=1, source_target_pairs={{0,4},{4,8},{8,12},{12,16},{16,20},{20,24},{24,28},{1,5},{5,9},{9,... | collective-permute-start | bytes 1327112 | tf_op jit(solution)/shard_map/ppermute | solution.py:12
  222.1 12.1 %collective-permute-start = (bf16[144,1536]{1,0:T(8,128)(2,1)S(1)}, bf16[144,1536]{1,0:T(8,128)(2,1)S(1)}, u32[]{:S(2)}, u32[]{:S(2)}) collective-permute-start(bf16[144,1536]{1,0:T(8,128)(2,1)S(1)} %fusion.77), channel_id=1, source_target_pairs={{0,4},{4,8},{8,12},{12,16},{16,20},{20,24},{24,28},{1,5},{5,9},{9,... | collective-permute-start | bytes 1327112 | tf_op jit(solution)/shard_map/ppermute | solution.py:12
  (3 other events, 5.5 us)
Sparse Core Ops, SparseCore 0:
  82.2 135.3 all-reduce.2
where the time goes:
time: 243 us
  waiting for transfers between devices  137 us (56%)
  matrix products  53.9 us (22%)
  local copies, waits for them, and re-layouts  15.9 us (7%)
  between operations  14.4 us (6%)
  other arithmetic  14.3 us (6%)
  starting transfers between devices  7.26 us (3%)
    psum x1, waiting for transfers between devices, per_device(): lax.psum(forward_term.astype(jnp.bfloat16), 'tensor').astype(jnp.float32)  101 us
    ppermute x3, waiting for transfers between devices, from_partner(): return lax.ppermute(value, axis, pairs)  29.4 us
    dot_general x9, matrix products, project(): jnp.dot(normed, weight, preferred_element_type=jnp.float32)  22 us
    dot_general x4, matrix products, head_block(): jnp.einsum('gqk,kgh->qgh', weights_bf.astype(jnp.float32), value_rows.ast...  10.9 us
    ppermute x2, waiting for transfers between devices, passed_along(): return lax.ppermute(value, axis, pairs)  6.88 us
    convert_element_type x6, local copies, waits for them, and re-layouts, project(): return jnp.dot(normed, weight, preferred_element_type=jnp.float32).astype...  6.81 us
    dot_general x2, matrix products, head_block(): jnp.dot(attended, w_out, preferred_element_type=jnp.float32)  6.64 us
    dot_general x3, matrix products, head_block(): jnp.einsum('qgh,kgh->gqk', queries.astype(jnp.float32), key_rows.astype(j...  5.95 us
  transfers between devices with their start and end apart: 6, of which 5 were waited for; matrix products, arithmetic and copies ran while one was open for 3% of the time, Pallas kernels for 0%

commit v1 on v0

--- a/solution.py
+++ b/solution.py
@@ -12,10 +12,9 @@
     return lax.ppermute(value, axis, pairs)
 
 
-def from_partner(value, axis, distance):
-    mask = 2**distance
-    pairs = [(source, source ^ mask) for source in range(lax.axis_size(axis))]
-    return lax.ppermute(value, axis, pairs)
+def mirror_exchange(value, axis):
+    peers = lax.axis_size(axis)
+    return lax.ppermute(value, axis, [(i, peers - 1 - i) for i in range(peers)])
 
 
 def rms_norm(activation, gain_vec):
@@ -106,24 +105,19 @@
         attended, cotangent, (((0,), (0,)), ((), ())), preferred_element_type=jnp.float32
     )
     backward_term = input_grad.astype(jnp.float32)
-    whole_forward, whole_backward = (
-        lax.psum(forward_term.astype(jnp.bfloat16), "tensor").astype(jnp.float32),
-        lax.psum(backward_term.astype(jnp.bfloat16), "tensor").astype(jnp.float32),
-    )
-    summed_forward = lax.dynamic_slice_in_dim(whole_forward, row_start, share_rows, 0)
-    summed_backward = lax.dynamic_slice_in_dim(whole_backward, row_start, share_rows, 0)
+    summed_forward = lax.psum_scatter(
+        forward_term.astype(jnp.bfloat16), "tensor", scatter_dimension=0, tiled=True
+    ).astype(jnp.float32)
+    summed_backward = lax.psum_scatter(
+        backward_term.astype(jnp.bfloat16), "tensor", scatter_dimension=0, tiled=True
+    ).astype(jnp.float32)
     forward_rows = lax.dynamic_slice_in_dim(forward_in, row_start, share_rows, 0)
     cotangent_rows = lax.dynamic_slice_in_dim(cotangent, row_start, share_rows, 0)
     section_rows = (forward_rows.astype(jnp.float32) + summed_forward).astype(jnp.bfloat16)
     grad_rows = (cotangent_rows.astype(jnp.float32) + summed_backward).astype(jnp.bfloat16)
-    moved_section, moved_grad = passed_along((section_rows, grad_rows), "pipe", 1)
-    bit_total = lax.axis_size("pipe").bit_length() - 1
-    bit_order = list(range(bit_total))
-    mirrored = weight_grad
-    for bit_index in bit_order:
-        mirrored = from_partner(mirrored.astype(jnp.bfloat16), "pipe", bit_index).astype(
-            mirrored.dtype
-        )
+    moved_section = passed_along(section_rows, "pipe", 1)
+    moved_grad = passed_along(grad_rows, "pipe", 1)
+    mirrored = mirror_exchange(weight_grad.astype(jnp.bfloat16), "pipe").astype(jnp.float32)
     return (moved_section[None], moved_grad[None], mirrored[None])
 
 

time: 243 us -> 155 us (0.64)
  waiting for transfers between devices: 137 us -> 44.2 us
  matrix products: 53.9 us -> 57.9 us
    psum x1 -> x0, waiting for transfers between devices: 101 us -> none  [per_device(): lax.psum(forward_term.astype(jnp.bfloat16), 'tensor').astype(jnp.float32)]
    reduce_scatter x0 -> x2, waiting for transfers between devices: none -> 37.3 us  [the longest x1 37.1 us: per_device(): lax.psum_scatter(forward_term.astype(jnp.bfloat16), 'tensor', scatter_dim...]
    ppermute x3 -> x1, waiting for transfers between devices: 29.4 us -> 0.01 us  [mirror_exchange(): return lax.ppermute(value, axis, [(i, peers - 1 - i) for i in range(peers)])]
    dot_general x9, matrix products: 22 us -> 26.5 us  [project(): jnp.dot(normed, weight, preferred_element_type=jnp.float32)]
  transfers between devices with their start and end apart: 6 -> 5, of which waited for: 5 -> 3; matrix products, arithmetic and copies ran while one was open for 3% -> 28% of each run, Pallas kernels for 0% -> 0%
where the time goes in v1:
time: 155 us; the launch traced here: 154 us
  matrix products  57.9 us (37%)
  waiting for transfers between devices  44.2 us (29%)
  local copies, waits for them, and re-layouts  15.9 us (10%)
  other arithmetic  15.8 us (10%)
  between operations  14.4 us (9%)
  starting transfers between devices  5.51 us (4%)
    reduce_scatter x1, waiting for transfers between devices, per_device(): lax.psum_scatter(forward_term.astype(jnp.bfloat16), 'tensor', scatter_dim...  37.1 us
    dot_general x9, matrix products, project(): jnp.dot(normed, weight, preferred_element_type=jnp.float32)  26.5 us
    dot_general x4, matrix products, head_block(): jnp.einsum('gqk,kgh->qgh', weights_bf.astype(jnp.float32), value_rows.ast...  10.9 us
    ppermute x2, waiting for transfers between devices, passed_along(): return lax.ppermute(value, axis, pairs)  6.89 us
    convert_element_type x6, local copies, waits for them, and re-layouts, project(): return jnp.dot(normed, weight, preferred_element_type=jnp.float32).astype...  6.82 us
    dot_general x2, matrix products, head_block(): jnp.dot(attended, w_out, preferred_element_type=jnp.float32)  6.49 us
    dot_general x3, matrix products, head_block(): jnp.einsum('qgh,kgh->gqk', queries.astype(jnp.float32), key_rows.astype(j...  5.95 us
    sub x1, matrix products, head_block(): weights = jnp.where(keep_mask[None], jnp.exp(scores - row_max), 0.0)  5.55 us
  transfers between devices with their start and end apart: 5, of which 3 were waited for; matrix products, arithmetic and copies ran while one was open for 28% of the time, Pallas kernels for 0%

profile of v1, /device:TPU:4, one launch (start us, length us, event | category | flops | bytes accessed | tf_op | source)
XLA Modules:
  0.0 153.7 jit_solution(10542465932247358246)
XLA Ops:
  8.0 1.9 %fusion.13 = f32[576]{0:T(1024)S(1)} fusion(bf16[1,576,1536]{2,1,0:T(8,128)(2,1)} %param.11), kind=kLoop, calls=%fused_computation.28 | loop fusion | flops 2653632 | bytes 1771776 | tf_op jit(solution)/shard_map/jvp()/reduce_sum | solution.py:22
  9.9 3.1 %convolution_convert_fusion.10 = bf16[576,384]{1,0:T(8,128)(2,1)S(1)} fusion(bf16[2,1,1536,384]{3,2,1,0:T(8,128)(2,1)} %param.16, bf16[1,576,1536]{2,1,0:T(8,128)(2,1)} %param.11, f32[1536]{0:T(1024)S(1)} %get-tuple-element.3, f32[576]{0:T(1024)S(1)} %fusion.80), kind=kOutput, calls=%fused_computation.75 | convolution fusion | flops 683237376 | bytes 3399936 | tf_op jit(solution)/shard_map/jvp()/dot_general | solution.py:41
  13.3 2.6 %convolution_convert_fusion.9 = bf16[576,384]{1,0:T(8,128)(2,1)S(1)} fusion(bf16[2,1,1536,384]{3,2,1,0:T(8,128)(2,1)} %param.17, bf16[1,576,1536]{2,1,0:T(8,128)(2,1)S(1)} %copy-done.1, f32[1536]{0:T(1024)S(1)} %get-tuple-element.3, f32[576]{0:T(1024)S(1)} %fusion.80), kind=kOutput, calls=%fused_computation.74 | convolution fusion | flops 683237376 | bytes 3399936 | tf_op jit(solution)/shard_map/jvp()/dot_general | solution.py:41
  17.5 2.1 %fusion.96 = (f32[3,576]{1,0:T(4,128)S(1)}, f32[3,576,576]{1,2,0:T(8,128)S(1)}) fusion(bf16[576,3,128]{0,2,1:T(8,128)(2,1)S(1)} %bitcast.130, bf16[576,3,128]{0,2,1:T(8,128)(2,1)} %bitcast.132, pred[576,576]{0,1:T(8,128)(4,1)S(1)} %fusion.41), kind=kOutput, calls=%fused_computation.132 | convolution fusion | flops 257788224 | bytes 5204736 | tf_op jit(solution)/shard_map/jvp(qgh,kgh->gqk)/dot_general | solution.py:49
  24.3 2.9 %fusion.43 = bf16[576,384]{1,0:T(8,128)(2,1)S(1)} fusion(bf16[1,576,1536]{2,1,0:T(8,128)(2,1)} %param.12, bf16[2,1,384,1536]{3,2,1,0:T(8,128)(2,1)} %param.19), kind=kOutput, calls=%fused_computation.67 | convolution fusion | flops 679698432 | bytes 3391488 | tf_op jit(solution)/shard_map/transpose(jvp())/dot_general | solution.py:60
  27.5 5.0 %convert_reduce_fusion = (f32[3,576]{1,0:T(4,128)S(1)}, pred[3,576,576]{1,2,0:T(32,128)(4,1)S(1)}, f32[3,576]{1,0:T(4,128)S(1)}, bf16[3,576,576]{1,2,0:T(8,128)(2,1)S(1)}) fusion(f32[3,576,576]{1,2,0:T(8,128)} %copy-done, f32[3,576]{1,0:T(4,128)S(1)} %get-tuple-element.13, pred[576,576]{0,1:T(8,128)(4,1)S(1)} %fusion.41, ...), kind=kOutput, calls=%fused_computation.10 | convolution fusion | flops 264753792 | bytes 8211456 | tf_op jit(solution)/shard_map/transpose(jvp(gqk,kgh->qgh))/dot_general | solution.py:56
  32.6 2.1 %fusion.93 = (f32[3,576]{1,0:T(4,128)S(1)}, f32[3,576,576]{1,2,0:T(8,128)S(1)}, bf16[3,576,576]{1,2,0:T(8,128)(2,1)S(1)}) fusion(f32[3,576,576]{1,2,0:T(8,128)S(1)} %bitcast.125, f32[3,576]{1,0:T(4,128)S(1)} %get-tuple-element.13, f32[3,576]{1,0:T(4,128)S(1)} %neg.9, f32[3,576]{1,0:T(4,128)S(1)} %fusion.21, bf16[3,576,576]{1,2,0:T(8,128)(2,1)S(1)} %get-tuple-element.15, ...), kind=kLoop, calls=%fused_computation.130 | loop fusion | flops 9951552 | bytes 12303360 | tf_op jit(solution)/shard_map/transpose(jvp())/reduce_sum | solution.py:54
  36.4 2.1 %fusion.52 = bf16[576,3,128]{2,0,1:T(8,128)(2,1)} fusion(bf16[576,3,128]{0,2,1:T(8,128)(2,1)S(1)} %bitcast.131, f32[3,576,576]{1,2,0:T(8,128)S(1)} %get-tuple-element.6, pred[3,576,576]{1,2,0:T(32,128)(4,1)S(1)} %get-tuple-element.8, f32[3,576]{1,0:T(4,128)S(1)} %negate_divide_fusion, pred[576,576]{0,1:T(8,128)(4,1)S(1)} %fusion.41), kind=kOutput, calls=%fused_computation.82 | convolution fusion | flops 259006464 | bytes 6200064 | tf_op jit(solution)/shard_map/transpose(jvp(qgh,kgh->gqk))/dot_general | solution.py:49
  40.8 3.7 %convolution_convert_fusion.1 = bf16[576,1536]{1,0:T(8,128)(2,1)} fusion(bf16[576,384]{0,1:T(8,128)(2,1)S(1)} %bitcast.139, bf16[2,1,1536,384]{3,2,1,0:T(8,128)(2,1)} %param.17), kind=kOutput, calls=%fused_computation.36 | convolution fusion | flops 680361984 | bytes 3391488 | tf_op jit(solution)/shard_map/transpose(jvp())/dot_general | solution.py:41
  46.2 3.3 %fusion.19 = bf16[576,1536]{1,0:T(8,128)(2,1)S(1)} fusion(bf16[576,1536]{1,0:T(8,128)(2,1)} %convolution_convert_fusion.1, bf16[576,384]{0,1:T(8,128)(2,1)} %bitcast.138, bf16[2,1,1536,384]{3,2,1,0:T(8,128)(2,1)} %param.18), kind=kOutput, calls=%fused_computation.39 | convolution fusion | flops 681246720 | bytes 5210112 | tf_op jit(solution)/shard_map/transpose(jvp())/dot_general | solution.py:41
  51.1 2.1 %fusion.17 = bf16[576,1536]{1,0:T(8,128)(2,1)} fusion(bf16[1,576,1536]{2,1,0:T(8,128)(2,1)S(1)} %copy-done.2, bf16[576,1536]{1,0:T(8,128)(2,1)S(1)} %get-tuple-element.17, f32[576]{0:T(1024)S(1)} %multiply_multiply_fusion, f32[576]{0:T(1024)S(1)} %fusion.80, f32[1536]{0:T(1024)S(1)} %get-tuple-element.3), kind=kLoop, calls=%fused_computation.32 | loop fusion | flops 7077888 | bytes 5319168 | tf_op jit(solution)/shard_map/transpose(jvp())/convert_element_type | solution.py:21
  55.5 3.7 %convolution_convert_fusion.12 = bf16[576,384]{1,0:T(8,128)(2,1)} fusion(bf16[2,1,1536,384]{3,2,1,0:T(8,128)(2,1)} %param.16, bf16[1,576,1536]{2,1,0:T(8,128)(2,1)} %param.10, f32[1536]{0:T(1024)S(1)} %get-tuple-element.4, f32[576]{0:T(1024)S(1)} %add_rsqrt_fusion), kind=kOutput, calls=%fused_computation.77 | convolution fusion | flops 683237376 | bytes 3399936 | tf_op jit(solution)/shard_map/dot_general | solution.py:41
  60.5 3.9 %convolution_convert_fusion.11 = bf16[576,384]{1,0:T(8,128)(2,1)} fusion(bf16[2,1,1536,384]{3,2,1,0:T(8,128)(2,1)} %param.17, bf16[1,576,1536]{2,1,0:T(8,128)(2,1)} %param.10, f32[1536]{0:T(1024)S(1)} %get-tuple-element.4, f32[576]{0:T(1024)S(1)} %add_rsqrt_fusion), kind=kOutput, calls=%fused_computation.76 | convolution fusion | flops 683237376 | bytes 3399936 | tf_op jit(solution)/shard_map/dot_general | solution.py:41
  64.3 2.0 %copy.54 = bf16[576,384]{0,1:T(8,128)(2,1)} copy(bf16[576,384]{1,0:T(8,128)(2,1)} %convolution_convert_fusion.11) | data formatting | bytes 884736 | tf_op jit(solution)/shard_map/convert_element_type | solution.py:42
  66.5 3.7 %convolution_convert_fusion.13 = bf16[576,384]{1,0:T(8,128)(2,1)} fusion(bf16[2,1,1536,384]{3,2,1,0:T(8,128)(2,1)} %param.18, bf16[1,576,1536]{2,1,0:T(8,128)(2,1)} %param.10, f32[1536]{0:T(1024)S(1)} %get-tuple-element.4, f32[576]{0:T(1024)S(1)} %add_rsqrt_fusion), kind=kOutput, calls=%fused_computation.78 | convolution fusion | flops 683237376 | bytes 3399936 | tf_op jit(solution)/shard_map/dot_general | solution.py:41
  70.2 2.0 %copy.52 = bf16[576,384]{0,1:T(8,128)(2,1)} copy(bf16[576,384]{1,0:T(8,128)(2,1)} %convolution_convert_fusion.13) | data formatting | bytes 884736 | tf_op jit(solution)/shard_map/convert_element_type | solution.py:42
  73.3 5.6 %fusion.95 = (f32[3,576]{1,0:T(4,128)S(1)}, f32[3,576,576]{1,2,0:T(8,128)}) fusion(pred[576,576]{0,1:T(8,128)(4,1)} %fusion.42, bf16[576,3,128]{0,2,1:T(8,128)(2,1)S(1)} %bitcast.134, bf16[576,3,128]{0,2,1:T(8,128)(2,1)} %bitcast.136), kind=kOutput, calls=%fused_computation.131 | convolution fusion | flops 259781184 | bytes 5204736 | tf_op jit(solution)/shard_map/sub | solution.py:54
  78.9 4.2 %fusion.53 = bf16[576,3,128]{2,0,1:T(8,128)(2,1)} fusion(bf16[576,3,128]{0,2,1:T(8,128)(2,1)} %bitcast.137, f32[3,576,576]{1,2,0:T(8,128)} %get-tuple-element.12, f32[3,576]{1,0:T(4,128)S(1)} %get-tuple-element.11), kind=kOutput, calls=%fused_computation.83 | convolution fusion | flops 257015808 | bytes 4872960 | tf_op jit(solution)/shard_map/gqk,kgh->qgh/dot_general | solution.py:56
  84.3 3.6 %convolution_convert_fusion.3 = bf16[576,1536]{1,0:T(8,128)(2,1)} fusion(bf16[576,384]{0,1:T(8,128)(2,1)S(1)} %bitcast.140, bf16[2,1,384,1536]{3,2,1,0:T(8,128)(2,1)} %param.19), kind=kOutput, calls=%fused_computation.38 | convolution fusion | flops 680361984 | bytes 3391488 | tf_op jit(solution)/shard_map/dot_general | solution.py:60
  89.2 2.6 %convolution_convert_fusion.4 = bf16[384,1536]{1,0:T(8,128)(2,1)S(1)} fusion(bf16[576,384]{0,1:T(8,128)(2,1)S(1)} %bitcast.141, bf16[1,576,1536]{2,1,0:T(8,128)(2,1)} %param.12), kind=kOutput, calls=%fused_computation.44 | convolution fusion | flops 680067072 | bytes 3391488 | tf_op jit(solution)/shard_map/dot_general | solution.py:104
  94.3 2.2 %collective-permute-start.1 = (bf16[144,1536]{1,0:T(8,128)(2,1)S(1)}, bf16[144,1536]{1,0:T(8,128)(2,1)S(1)}, u32[]{:S(2)}, u32[]{:S(2)}) collective-permute-start(bf16[144,1536]{1,0:T(8,128)(2,1)S(1)} %fusion.76), channel_id=1, source_target_pairs={{0,4},{4,8},{8,12},{12,16},{16,20},{20,24},{24,28},{1,5},{5,9},{9,... | collective-permute-start | bytes 1327112 | tf_op jit(solution)/shard_map/ppermute | solution.py:12
  96.5 37.1 %reduce-scatter.3.cloned.1.call-done = bf16[144,1536]{1,0:T(8,128)(2,1)} async-done(((bf16[576,1536]{1,0:T(8,128)(2,1)}), bf16[144,1536]{1,0:T(8,128)(2,1)}) %reduce-scatter.3.cloned.1.call-update) | async-done | bytes 442384 | tf_op jit(solution)/shard_map/reduce_scatter | solution.py:108
  134.8 1.9 %collective-permute-start = (bf16[144,1536]{1,0:T(8,128)(2,1)S(1)}, bf16[144,1536]{1,0:T(8,128)(2,1)S(1)}, u32[]{:S(2)}, u32[]{:S(2)}) collective-permute-start(bf16[144,1536]{1,0:T(8,128)(2,1)S(1)} %fusion.77), channel_id=1, source_target_pairs={{0,4},{4,8},{8,12},{12,16},{16,20},{20,24},{24,28},{1,5},{5,9},{9,... | collective-permute-start | bytes 1327112 | tf_op jit(solution)/shard_map/ppermute | solution.py:12
  138.5 6.9 %collective-permute-done = bf16[144,1536]{1,0:T(8,128)(2,1)S(1)} collective-permute-done((bf16[144,1536]{1,0:T(8,128)(2,1)S(1)}, bf16[144,1536]{1,0:T(8,128)(2,1)S(1)}, u32[]{:S(2)}, u32[]{:S(2)}) %collective-permute-start) | collective-permute-done | bytes 442400 | tf_op jit(solution)/shard_map/ppermute | solution.py:12
  (74 shorter events, 29.2 us)
Async XLA Ops:
  7.2 85.9 %reduce-scatter.5.cloned.1.call-start = ((), (), s32[]{:S(2)}) async-start(), calls=%async_computation.3 | async-start | bytes 2211840 | tf_op jit(solution)/shard_map/reduce_scatter | solution.py:111
  9.9 3.3 %copy-start.1 = (bf16[1,576,1536]{2,1,0:T(8,128)(2,1)S(1)}, bf16[1,576,1536]{2,1,0:T(8,128)(2,1)}, u32[]{:S(2)}) copy-start(bf16[1,576,1536]{2,1,0:T(8,128)(2,1)} %param.11) | copy-start | bytes 5308420
  13.3 4.2 %copy-start.5 = (bf16[576,384]{0,1:T(8,128)(2,1)}, bf16[576,384]{0,1:T(8,128)(2,1)S(1)}, u32[]{:S(2)}) copy-start(bf16[576,384]{0,1:T(8,128)(2,1)S(1)} %copy.61) | copy-start | bytes 1327108
  13.3 3.6 %copy-start.11 = (s32[1,8]{1,0:T(1,128)S(1)}, s32[1,8]{1,0:T(1,128)}, u32[]{:S(2)}) copy-start(s32[1,8]{1,0:T(1,128)} %param.14) | copy-start | bytes 100
  19.6 2.3 %copy-start = (f32[3,576,576]{1,2,0:T(8,128)}, f32[3,576,576]{1,2,0:T(8,128)S(1)}, u32[]{:S(2)}) copy-start(f32[3,576,576]{1,2,0:T(8,128)S(1)} %get-tuple-element.14) | copy-start | bytes 11943940
  19.6 3.3 %copy-start.10 = (bf16[2,1,1536,384]{3,2,1,0:T(8,128)(2,1)S(1)}, bf16[2,1,1536,384]{3,2,1,0:T(8,128)(2,1)}, u32[]{:S(2)}) copy-start(bf16[2,1,1536,384]{3,2,1,0:T(8,128)(2,1)} %param.18) | copy-start | bytes 7077892
  27.4 5.1 %copy-start.3 = (bf16[576,384]{0,1:T(8,128)(2,1)}, bf16[576,384]{0,1:T(8,128)(2,1)S(1)}, u32[]{:S(2)}) copy-start(bf16[576,384]{0,1:T(8,128)(2,1)S(1)} %copy.60) | copy-start | bytes 1327108
  27.5 5.1 %slice-start = ((s8[4423680]{0:T(1024)(128)(4,1)}), s8[4194304]{0:T(1024)(128)(4,1)S(1)}, s32[]{:S(2)}) async-start(s8[4423680]{0:T(1024)(128)(4,1)} %bitcast.124), calls=%async_computation.4 | async-start | bytes 8388608
  27.5 5.1 %slice-start.1 = ((s8[4423680]{0:T(1024)(128)(4,1)}), s8[229376]{0:T(1024)(128)(4,1)S(1)}, s32[]{:S(2)}) async-start(s8[4423680]{0:T(1024)(128)(4,1)} %bitcast.124), calls=%async_computation.5 | async-start | bytes 458752
  32.6 2.1 %copy-start.7 = (bf16[576,384]{0,1:T(8,128)(2,1)S(1)}, bf16[576,384]{0,1:T(8,128)(2,1)}, u32[]{:S(2)}) copy-start(bf16[576,384]{0,1:T(8,128)(2,1)} %copy.62) | copy-start | bytes 1327108
  34.7 1.7 %copy-start.6 = (bf16[576,384]{0,1:T(8,128)(2,1)S(1)}, bf16[576,384]{0,1:T(8,128)(2,1)}, u32[]{:S(2)}) copy-start(bf16[576,384]{0,1:T(8,128)(2,1)} %copy-done.5) | copy-start | bytes 1327108
  40.8 3.7 %copy-start.4 = (bf16[576,384]{0,1:T(8,128)(2,1)S(1)}, bf16[576,384]{0,1:T(8,128)(2,1)}, u32[]{:S(2)}) copy-start(bf16[576,384]{0,1:T(8,128)(2,1)} %copy-done.3) | copy-start | bytes 1327108
  46.2 3.3 %copy-start.2 = (bf16[1,576,1536]{2,1,0:T(8,128)(2,1)S(1)}, bf16[1,576,1536]{2,1,0:T(8,128)(2,1)}, u32[]{:S(2)}) copy-start(bf16[1,576,1536]{2,1,0:T(8,128)(2,1)} %param.11) | copy-start | bytes 5308420
  46.2 3.3 %copy-start.8 = (bf16[576,3,128]{0,2,1:T(8,128)(2,1)S(1)}, bf16[576,3,128]{0,2,1:T(8,128)(2,1)}, u32[]{:S(2)}) copy-start(bf16[576,3,128]{0,2,1:T(8,128)(2,1)} %copy.74) | copy-start | bytes 1327108
  46.2 3.4 %copy-start.9 = (bf16[2,1,1536,384]{3,2,1,0:T(8,128)(2,1)S(1)}, bf16[2,1,1536,384]{3,2,1,0:T(8,128)(2,1)}, u32[]{:S(2)}) copy-start(bf16[2,1,1536,384]{3,2,1,0:T(8,128)(2,1)} %param.16) | copy-start | bytes 7077892
  53.3 80.3 %reduce-scatter.3.cloned.1.call-start = ((), (), s32[]{:S(2)}) async-start(), calls=%async_computation.2 | async-start | bytes 2211840 | tf_op jit(solution)/shard_map/reduce_scatter | solution.py:108
  60.4 5.9 %copy-start.12 = (s32[1,8]{1,0:T(1,128)S(1)}, s32[1,8]{1,0:T(1,128)}, u32[]{:S(2)}) copy-start(s32[1,8]{1,0:T(1,128)} %param.13) | copy-start | bytes 100
  91.7 45.0 %collective-permute-start.2 = (bf16[384,1536]{1,0:T(8,128)(2,1)S(1)}, bf16[384,1536]{1,0:T(8,128)(2,1)S(1)}, u32[]{:S(2)}, u32[]{:S(2)}) collective-permute-start(bf16[384,1536]{1,0:T(8,128)(2,1)S(1)} %convolution_convert_fusion.4), channel_id=1, source_target_pairs={{0,28},{4,24},{8,20},{12,16},{16,12},{20,8},{24,4},{28,0},{1,29},{... | collective-permute-start | bytes 3538952 | tf_op jit(solution)/shard_map/ppermute | solution.py:17
  94.3 44.2 %collective-permute-start.1 = (bf16[144,1536]{1,0:T(8,128)(2,1)S(1)}, bf16[144,1536]{1,0:T(8,128)(2,1)S(1)}, u32[]{:S(2)}, u32[]{:S(2)}) collective-permute-start(bf16[144,1536]{1,0:T(8,128)(2,1)S(1)} %fusion.76), channel_id=1, source_target_pairs={{0,4},{4,8},{8,12},{12,16},{16,20},{20,24},{24,28},{1,5},{5,9},{9,... | collective-permute-start | bytes 1327112 | tf_op jit(solution)/shard_map/ppermute | solution.py:12
  134.8 10.5 %collective-permute-start = (bf16[144,1536]{1,0:T(8,128)(2,1)S(1)}, bf16[144,1536]{1,0:T(8,128)(2,1)S(1)}, u32[]{:S(2)}, u32[]{:S(2)}) collective-permute-start(bf16[144,1536]{1,0:T(8,128)(2,1)S(1)} %fusion.77), channel_id=1, source_target_pairs={{0,4},{4,8},{8,12},{12,16},{16,20},{20,24},{24,28},{1,5},{5,9},{9,... | collective-permute-start | bytes 1327112 | tf_op jit(solution)/shard_map/ppermute | solution.py:12
Sparse Core Ops, SparseCore 0:
  53.4 39.5 reduce-scatter.4
  96.0 37.4 reduce-scatter.2

commit v2 on v1

v2 whole, which is shorter than its diff:
```python
import jax
import jax.numpy as jnp
from jax import lax
from jax.experimental import pallas as pl
from jax.experimental.pallas import tpu as pltpu
from jax.sharding import PartitionSpec as P

HEAD_DIM = 128
MOST = 192
VMEM_LIMIT = 48 * 1024 * 1024


def passed_along(value, axis, by):
    peers = lax.axis_size(axis)
    pairs = [(i, i + by) for i in range(peers) if 0 <= i + by < peers]
    return lax.ppermute(value, axis, pairs)


def mirror_exchange(value, axis):
    peers = lax.axis_size(axis)
    return lax.ppermute(value, axis, [(i, peers - 1 - i) for i in range(peers)])


def doc_start(lengths_ref, first_row, row_count):
    position = lax.broadcasted_iota(jnp.int32, (row_count, 1), 0) + first_row
    start = jnp.zeros((row_count, 1), jnp.int32)
    end = jnp.int32(0)
    for doc in range(lengths_ref.shape[1]):
        end = end + lengths_ref[0, doc]
        start = jnp.where(position >= end, end, start)
    return position, start


def dot_nn(left, right):
    return jnp.dot(left, right, preferred_element_type=jnp.float32)


def dot_nt(left, right):
    return lax.dot_general(
        left, right, (((1,), (1,)), ((), ())), preferred_element_type=jnp.float32
    )


def dot_tn(left, right):
    return lax.dot_general(
        left, right, (((0,), (0,)), ((), ())), preferred_element_type=jnp.float32
    )


def start_copies(pairs, sems):
    copies = []
    for index, (source, target) in enumerate(pairs):
        copy = pltpu.make_async_copy(source, target, sems.at[index])
        copy.start()
        copies.append(copy)
    return copies


def normed_rows(x_ref, gain, rows):
    widened = x_ref[rows, :].astype(jnp.float32)
    mean_square = jnp.mean(widened * widened, axis=-1, keepdims=True)
    scale = lax.rsqrt(mean_square + 1e-05)
    return (widened * scale * gain).astype(jnp.bfloat16), scale


def score_block(queries, key_rows, keep):
    scores = dot_nt(queries, key_rows) * HEAD_DIM ** (-0.5)
    scores = jnp.where(keep, scores, -1e30)
    weights = jnp.exp(scores - jnp.max(scores, axis=-1, keepdims=True))
    return weights, 1.0 / jnp.sum(weights, axis=-1, keepdims=True)


def window_mask(lengths_ref, first_row, first_key, last_key):
    position, start = doc_start(lengths_ref, first_row, MOST)
    keys = lax.broadcasted_iota(jnp.int32, (MOST, last_key - first_key), 1) + first_key
    return (keys >= start) & (keys <= position)


def forward_kernel(
    lengths_ref, gain_ref, x_hbm, wq_hbm, wk_hbm, wv_hbm, wo_hbm, out_ref,
    x_ref, w_ref, wo_ref, qkv_ref, sems,
):
    width = wq_hbm.shape[3]
    copies = start_copies(
        [
            (x_hbm.at[0], x_ref),
            (wq_hbm.at[0, 0], w_ref.at[:, 0:width]),
            (wk_hbm.at[0, 0], w_ref.at[:, width : 2 * width]),
            (wv_hbm.at[0, 0], w_ref.at[:, 2 * width : 3 * width]),
            (wo_hbm.at[0, 0], wo_ref),
        ],
        sems,
    )
    gain = gain_ref[0].astype(jnp.float32)
    copies[0].wait()
    blocks = x_ref.shape[0] // MOST
    for block in range(blocks):
        low, high = block * MOST, (block + 1) * MOST
        normed, unused = normed_rows(x_ref, gain, slice(low, high))
        if block == 0:
            for copy in copies[1:4]:
                copy.wait()
        qkv_ref[low:high, :] = dot_nn(normed, w_ref[...]).astype(jnp.bfloat16)
    for block in range(blocks):
        low, high = block * MOST, (block + 1) * MOST
        key_low = max(0, low - MOST)
        keep = window_mask(lengths_ref, low, key_low, high)
        parts = []
        for head in range(width // HEAD_DIM):
            at = head * HEAD_DIM
            weights, inverse = score_block(
                qkv_ref[low:high, at : at + HEAD_DIM],
                qkv_ref[key_low:high, width + at : width + at + HEAD_DIM],
                keep,
            )
            mixed = dot_nn(
                (weights * inverse).astype(jnp.bfloat16),
                qkv_ref[key_low:high, 2 * width + at : 2 * width + at + HEAD_DIM],
            )
            parts.append(mixed.astype(jnp.bfloat16))
        attended = jnp.concatenate(parts, axis=1)
        if block == 0:
            copies[4].wait()
        out_ref[low:high, :] = dot_nn(attended, wo_ref[...]).astype(jnp.bfloat16)


def backward_kernel(
    lengths_ref, gain_ref, x_hbm, c_hbm, wq_hbm, wk_hbm, wv_hbm, wo_hbm, out_ref, grad_ref,
    x_ref, c_ref, w_ref, wo_ref, qkv_ref, dqkv_ref, att_ref, sems,
):
    width = wq_hbm.shape[3]
    copies = start_copies(
        [
            (x_hbm.at[0], x_ref),
            (wq_hbm.at[1, 0], w_ref.at[:, 0:width]),
            (wk_hbm.at[1, 0], w_ref.at[:, width : 2 * width]),
            (wv_hbm.at[1, 0], w_ref.at[:, 2 * width : 3 * width]),
            (c_hbm.at[0], c_ref),
            (wo_hbm.at[1, 0], wo_ref),
        ],
        sems,
    )
    gain = gain_ref[1].astype(jnp.float32)
    copies[0].wait()
    blocks = x_ref.shape[0] // MOST
    heads = width // HEAD_DIM
    scales = []
    for block in range(blocks):
        low, high = block * MOST, (block + 1) * MOST
        normed, scale = normed_rows(x_ref, gain, slice(low, high))
        scales.append(scale)
        if block == 0:
            for copy in copies[1:4]:
                copy.wait()
        qkv_ref[low:high, :] = dot_nn(normed, w_ref[...]).astype(jnp.bfloat16)
    copies[4].wait()
    copies[5].wait()
    carried = {}
    for block in range(blocks):
        low, high = block * MOST, (block + 1) * MOST
        key_low = max(0, low - MOST)
        keep = window_mask(lengths_ref, low, key_low, high)
        d_attended = dot_nt(c_ref[low:high, :], wo_ref[...]).astype(jnp.bfloat16)
        for head in range(heads):
            at = head * HEAD_DIM
            cols = [slice(part * width + at, part * width + at + HEAD_DIM) for part in range(3)]
            queries = qkv_ref[low:high, cols[0]]
            key_rows = qkv_ref[key_low:high, cols[1]]
            value_rows = qkv_ref[key_low:high, cols[2]]
            weights, inverse = score_block(queries, key_rows, keep)
            probs = weights * inverse
            probs_bf = probs.astype(jnp.bfloat16)
            mixed = dot_nn(probs_bf, value_rows)
            att_ref[low:high, at : at + HEAD_DIM] = mixed.astype(jnp.bfloat16)
            d_mixed = d_attended[:, at : at + HEAD_DIM]
            d_probs = dot_nt(d_mixed, value_rows)
            delta = jnp.sum(mixed * d_mixed.astype(jnp.float32), axis=-1, keepdims=True)
            d_scores = (probs * (d_probs - delta) * HEAD_DIM ** (-0.5)).astype(jnp.bfloat16)
            dqkv_ref[low:high, cols[0]] = dot_nn(d_scores, key_rows).astype(jnp.bfloat16)
            d_keys = dot_tn(d_scores, queries)
            d_values = dot_tn(probs_bf, d_mixed)
            if block > 0:
                past_keys, past_values = carried[head]
                dqkv_ref[key_low:low, cols[1]] = (past_keys + d_keys[:MOST]).astype(jnp.bfloat16)
                dqkv_ref[key_low:low, cols[2]] = (past_values + d_values[:MOST]).astype(
                    jnp.bfloat16
                )
                d_keys, d_values = d_keys[MOST:], d_values[MOST:]
            if block == blocks - 1:
                dqkv_ref[low:high, cols[1]] = d_keys.astype(jnp.bfloat16)
                dqkv_ref[low:high, cols[2]] = d_values.astype(jnp.bfloat16)
            carried[head] = (d_keys, d_values)
    for block in range(blocks):
        low, high = block * MOST, (block + 1) * MOST
        d_normed = dot_nt(dqkv_ref[low:high, :], w_ref[...]) * gain
        widened = x_ref[low:high, :].astype(jnp.float32)
        scale = scales[block]
        pull = jnp.mean(d_normed * widened, axis=-1, keepdims=True) * scale * scale * scale
        out_ref[low:high, :] = (d_normed * scale - widened * pull).astype(jnp.bfloat16)
    for head in range(heads):
        at = head * HEAD_DIM
        grad_ref[at : at + HEAD_DIM, :] = dot_tn(
            att_ref[:, at : at + HEAD_DIM], c_ref[...]
        ).astype(jnp.bfloat16)


SMEM_SPEC = pl.BlockSpec(memory_space=pltpu.SMEM)
VMEM_SPEC = pl.BlockSpec(memory_space=pltpu.VMEM)
ANY_SPEC = pl.BlockSpec(memory_space=pl.ANY)


def forward_term_of(lengths, gains, x, wq, wk, wv, wo):
    rows, wide, width = x.shape[1], x.shape[2], wq.shape[3]
    bf16 = jnp.bfloat16
    return pl.pallas_call(
        forward_kernel,
        out_shape=jax.ShapeDtypeStruct((rows, wide), bf16),
        in_specs=[SMEM_SPEC, VMEM_SPEC] + [ANY_SPEC] * 5,
        out_specs=VMEM_SPEC,
        scratch_shapes=[
            pltpu.VMEM((rows, wide), bf16),
            pltpu.VMEM((wide, 3 * width), bf16),
            pltpu.VMEM((width, wide), bf16),
            pltpu.VMEM((rows, 3 * width), bf16),
            pltpu.SemaphoreType.DMA((5,)),
        ],
        compiler_params=pltpu.CompilerParams(vmem_limit_bytes=VMEM_LIMIT),
        cost_estimate=pl.CostEstimate(
            flops=8 * rows * wide * width, bytes_accessed=8 * wide * (rows + width),
            transcendentals=rows * MOST,
        ),
        name="forward_section",
    )(lengths, gains, x, wq, wk, wv, wo)


def backward_terms_of(lengths, gains, x, c, wq, wk, wv, wo):
    rows, wide, width = x.shape[1], x.shape[2], wq.shape[3]
    bf16 = jnp.bfloat16
    return pl.pallas_call(
        backward_kernel,
        out_shape=(
            jax.ShapeDtypeStruct((rows, wide), bf16),
            jax.ShapeDtypeStruct((width, wide), bf16),
        ),
        in_specs=[SMEM_SPEC, VMEM_SPEC] + [ANY_SPEC] * 6,
        out_specs=(VMEM_SPEC, VMEM_SPEC),
        scratch_shapes=[
            pltpu.VMEM((rows, wide), bf16),
            pltpu.VMEM((rows, wide), bf16),
            pltpu.VMEM((wide, 3 * width), bf16),
            pltpu.VMEM((width, wide), bf16),
            pltpu.VMEM((rows, 3 * width), bf16),
            pltpu.VMEM((rows, 3 * width), bf16),
            pltpu.VMEM((rows, width), bf16),
            pltpu.SemaphoreType.DMA((6,)),
        ],
        compiler_params=pltpu.CompilerParams(vmem_limit_bytes=VMEM_LIMIT),
        cost_estimate=pl.CostEstimate(
            flops=16 * rows * wide * width, bytes_accessed=8 * wide * (rows + width),
            transcendentals=rows * MOST,
        ),
        name="backward_section",
    )(lengths, gains, x, c, wq, wk, wv, wo)


def per_device(
    fwd_inputs,
    bwd_inputs,
    bwd_cotangent,
    fwd_lengths,
    bwd_lengths,
    norm_gains,
    query_weight,
    key_weight,
    value_weight,
    out_weight,
):
    row_count = fwd_inputs.shape[1]
    share_rows = row_count // lax.axis_size("tensor")
    row_start = lax.axis_index("tensor") * share_rows
    forward_in = fwd_inputs[0]
    cotangent = bwd_cotangent[0]
    forward_term = forward_term_of(
        fwd_lengths, norm_gains, fwd_inputs, query_weight, key_weight, value_weight, out_weight
    )
    backward_term, weight_grad = backward_terms_of(
        bwd_lengths,
        norm_gains,
        bwd_inputs,
        bwd_cotangent,
        query_weight,
        key_weight,
        value_weight,
        out_weight,
    )
    summed_forward = lax.psum_scatter(
        forward_term, "tensor", scatter_dimension=0, tiled=True
    ).astype(jnp.float32)
    summed_backward = lax.psum_scatter(
        backward_term, "tensor", scatter_dimension=0, tiled=True
    ).astype(jnp.float32)
    forward_rows = lax.dynamic_slice_in_dim(forward_in, row_start, share_rows, 0)
    cotangent_rows = lax.dynamic_slice_in_dim(cotangent, row_start, share_rows, 0)
    section_rows = (forward_rows.astype(jnp.float32) + summed_forward).astype(jnp.bfloat16)
    grad_rows = (cotangent_rows.astype(jnp.float32) + summed_backward).astype(jnp.bfloat16)
    moved_section = passed_along(section_rows, "pipe", 1)
    moved_grad = passed_along(grad_rows, "pipe", 1)
    mirrored = mirror_exchange(weight_grad, "pipe").astype(jnp.float32)
    return (moved_section[None], moved_grad[None], mirrored[None])


def solution(mesh):
    placed = (
        P("pipe", None, None),
        P("pipe", None, None),
        P("pipe", None, None),
        P("pipe", None),
        P("pipe", None),
        P(None, "pipe", None),
        P(None, "pipe", None, "tensor"),
        P(None, "pipe", None, "tensor"),
        P(None, "pipe", None, "tensor"),
        P(None, "pipe", "tensor", None),
    )
    return jax.shard_map(
        per_device,
        mesh=mesh,
        in_specs=placed,
        out_specs=(P("pipe", "tensor", None), P("pipe", "tensor", None), P("pipe", "tensor", None)),
        check_vma=False,
    )
```

time: 155 us -> 122 us (0.79)
  matrix products: 57.9 us -> 0 us
  Pallas kernels: 0 us -> 27.3 us
  waiting for transfers between devices: 44.2 us -> 63.9 us
  other arithmetic: 15.8 us -> 4.19 us
  local copies, waits for them, and re-layouts: 15.9 us -> 7.23 us
    dot_general x19 -> x0, matrix products: 52.4 us -> none  [the longest x9 26.5 us: project(): jnp.dot(normed, weight, preferred_element_type=jnp.float32)]
    pallas_call x0 -> x2, Pallas kernels: none -> 27.3 us  [the longest x1 17.1 us: backward_terms_of(): pl.pallas_call(backward_kernel, out_shape=(jax.ShapeDtypeStruct((rows, wi...]
    reduce_scatter x2, waiting for transfers between devices: 37.3 us -> 57 us  [the longest x1 36.8 us: per_device(): lax.psum_scatter(backward_term, 'tensor', scatter_dimension=0, tiled=True)]
    convert_element_type x12 -> x0, local copies, waits for them, and re-layouts: 11.8 us -> none  [the longest x6 6.82 us: project(): return jnp.dot(normed, weight, preferred_element_type=jnp.float32).astype...]
    reduce_sum x6 -> x0, other arithmetic: 6.95 us -> none  [the longest x2 3.82 us: rms_norm(): mean_square = jnp.mean(widened * widened, axis=-1, keepdims=True)]
    sub x1 -> x0, matrix products: 5.55 us -> none  [head_block(): weights = jnp.where(keep_mask[None], jnp.exp(scores - row_max), 0.0)]
    unnamed x32 -> x13, local copies, waits for them, and re-layouts: 4.04 us -> 7.23 us
    convert_element_type x2 -> x0, other arithmetic: 2.94 us -> none  [the longest x1 2.14 us: rms_norm(): widened = activation.astype(jnp.float32)]
  transfers between devices with their start and end apart: 5 -> 5, of which waited for: 3 -> 3; matrix products, arithmetic and copies ran while one was open for 28% -> 3% of each run, Pallas kernels for 0% -> 14%
where the time goes in v2:
time: 122 us
  waiting for transfers between devices  63.9 us (52%)
  Pallas kernels  27.3 us (22%)
  between operations  14.1 us (12%)
  local copies, waits for them, and re-layouts  7.23 us (6%)
  starting transfers between devices  5.03 us (4%)
  other arithmetic  4.19 us (3%)
    reduce_scatter x1, waiting for transfers between devices, per_device(): lax.psum_scatter(backward_term, 'tensor', scatter_dimension=0, tiled=True)  36.8 us
    reduce_scatter x1, waiting for transfers between devices, per_device(): lax.psum_scatter(forward_term, 'tensor', scatter_dimension=0, tiled=True)  20.2 us
    pallas_call x1, Pallas kernels, backward_terms_of(): pl.pallas_call(backward_kernel, out_shape=(jax.ShapeDtypeStruct((rows, wi...  17.1 us
    pallas_call x1, Pallas kernels, forward_term_of(): pl.pallas_call(forward_kernel, out_shape=jax.ShapeDtypeStruct((rows, wide...  10.2 us
    unnamed x13, local copies, waits for them, and re-layouts  7.23 us
    ppermute x2, waiting for transfers between devices, passed_along(): return lax.ppermute(value, axis, pairs)  6.89 us
    ppermute x2, starting transfers between devices, passed_along(): return lax.ppermute(value, axis, pairs)  3.84 us
  transfers between devices with their start and end apart: 5, of which 3 were waited for; matrix products, arithmetic and copies ran while one was open for 3% of the time, Pallas kernels for 14%

profile of v2, /device:TPU:4, one launch (start us, length us, event | category | flops | bytes accessed | tf_op | source)
XLA Modules:
  0.0 121.8 jit_solution(10742964152837514967)
XLA Ops:
  7.2 0.0 reduce-scatter.3.cloned.1.call-start
  7.2 0.7 copy.13.gain_ref
  7.9 0.0 copy-start
  7.9 1.5 %copy-done = bf16[1,576,1536]{2,1,0:T(8,128)(2,1)S(1)} copy-done((bf16[1,576,1536]{2,1,0:T(8,128)(2,1)S(1)}, bf16[1,576,1536]{2,1,0:T(8,128)(2,1)}, u32[]{:S(2)}) %copy-start) | copy-done | bytes 1769496
  9.4 1.7 %copy-done.1 = bf16[2,1,1536,384]{3,2,1,0:T(8,128)(2,1)S(1)} copy-done((bf16[2,1,1536,384]{3,2,1,0:T(8,128)(2,1)S(1)}, bf16[2,1,1536,384]{3,2,1,0:T(8,128)(2,1)}, u32[]{:S(2)}) %copy-start.1) | copy-done | bytes 2359320
  11.1 0.7 copy-done.2
  11.7 10.2 %forward_section.1 = bf16[576,1536]{1,0:T(8,128)(2,1)} custom-call(s32[1,8]{1,0:T(1,128)S(1)} %copy-done.2, bf16[2,1,1536]{2,1,0:T(2,128)(2,1)S(1)} %copy.13.gain_ref, bf16[1,576,1536]{2,1,0:T(8,128)(2,1)S(1)} %copy-done, bf16[2,1,1536,384]{3,2,1,0:T(8,128)(2,1)S(1)} %copy-done.1, bf16[2,1,1536,384]{3,2,1,0:T(8,128)(2,1)} %wk_hbm.3, ...), custom_call_target="tpu_custom_call" | custom-call | flops 2717908992 | bytes 11796480 | tf_op jit(solution)/shard_map/forward_section/pallas_call | solution.py:215
  21.9 0.0 copy-start.3
  22.0 0.0 reduce-scatter.3.cloned.1.call-update
  22.0 0.2 reduce-scatter.5.cloned.1.call-start
  22.2 1.2 copy-done.3
  23.4 17.1 %backward_section.1 = (bf16[576,1536]{1,0:T(8,128)(2,1)}, bf16[384,1536]{1,0:T(8,128)(2,1)S(1)}) custom-call(s32[1,8]{1,0:T(1,128)S(1)} %copy-done.4, bf16[2,1,1536]{2,1,0:T(2,128)(2,1)S(1)} %copy.13.gain_ref, bf16[1,576,1536]{2,1,0:T(8,128)(2,1)S(1)} %copy-done.3, bf16[1,576,1536]{2,1,0:T(8,128)(2,1)} %c_hbm.1, bf16[2,1,1536,384]{3,2,1,0:T(8,128)(2,1)} %wq_hbm.3, ...), custom_call_target="tpu_custom_call" | custom-call | flops 5435817984 | bytes 11796480 | tf_op jit(solution)/shard_map/backward_section/pallas_call | solution.py:239
  40.5 0.0 reduce-scatter.5.cloned.1.call-update
  40.5 0.9 collective-permute-start.2
  41.5 20.2 %reduce-scatter.3.cloned.1.call-done = bf16[144,1536]{1,0:T(8,128)(2,1)} async-done(((bf16[576,1536]{1,0:T(8,128)(2,1)}), bf16[144,1536]{1,0:T(8,128)(2,1)}) %reduce-scatter.3.cloned.1.call-update) | async-done | bytes 442384 | tf_op jit(solution)/shard_map/reduce_scatter | solution.py:296
  61.7 1.2 %fusion.1 = bf16[144,1536]{1,0:T(8,128)(2,1)S(1)} fusion(bf16[144,1536]{1,0:T(8,128)(2,1)} %reduce-scatter.3.cloned.1.call-done, bf16[1,576,1536]{2,1,0:T(8,128)(2,1)} %x_hbm.2, s32[]{:T(128)S(6)} %select_n.4), kind=kLoop, calls=%fused_computation.4 | loop fusion | flops 884736 | bytes 1327108 | tf_op jit(solution)/shard_map/convert_element_type | solution.py:304
  63.0 1.9 %collective-permute-start = (bf16[144,1536]{1,0:T(8,128)(2,1)S(1)}, bf16[144,1536]{1,0:T(8,128)(2,1)S(1)}, u32[]{:S(2)}, u32[]{:S(2)}) collective-permute-start(bf16[144,1536]{1,0:T(8,128)(2,1)S(1)} %fusion.1), channel_id=1, source_target_pairs={{0,4},{4,8},{8,12},{12,16},{16,20},{20,24},{24,28},{1,5},{5,9},{9,... | collective-permute-start | bytes 1327112 | tf_op jit(solution)/shard_map/ppermute | solution.py:16
  64.9 36.8 %reduce-scatter.5.cloned.1.call-done = bf16[144,1536]{1,0:T(8,128)(2,1)} async-done(((bf16[576,1536]{1,0:T(8,128)(2,1)}), bf16[144,1536]{1,0:T(8,128)(2,1)}) %reduce-scatter.5.cloned.1.call-update) | async-done | bytes 442384 | tf_op jit(solution)/shard_map/reduce_scatter | solution.py:299
  101.7 1.2 %fusion = bf16[144,1536]{1,0:T(8,128)(2,1)S(1)} fusion(bf16[144,1536]{1,0:T(8,128)(2,1)} %reduce-scatter.5.cloned.1.call-done, bf16[1,576,1536]{2,1,0:T(8,128)(2,1)} %c_hbm.1, s32[]{:T(128)S(6)} %select_n.4), kind=kLoop, calls=%fused_computation.2 | loop fusion | flops 884736 | bytes 1327108 | tf_op jit(solution)/shard_map/convert_element_type | solution.py:305
  102.9 1.9 %collective-permute-start.1 = (bf16[144,1536]{1,0:T(8,128)(2,1)S(1)}, bf16[144,1536]{1,0:T(8,128)(2,1)S(1)}, u32[]{:S(2)}, u32[]{:S(2)}) collective-permute-start(bf16[144,1536]{1,0:T(8,128)(2,1)S(1)} %fusion), channel_id=1, source_target_pairs={{0,4},{4,8},{8,12},{12,16},{16,20},{20,24},{24,28},{1,5},{5,9},{9,... | collective-permute-start | bytes 1327112 | tf_op jit(solution)/shard_map/ppermute | solution.py:16
  104.9 1.7 %bitcast_convert_fusion = f32[1,384,1536]{2,1,0:T(8,128)} fusion(bf16[384,1536]{1,0:T(8,128)(2,1)S(1)} %collective-permute-done.2), kind=kLoop, calls=%fused_computation | loop fusion | flops 589824 | bytes 3538944 | tf_op jit(solution)/shard_map/broadcast_in_dim | solution.py:309
  106.6 6.9 %collective-permute-done.1 = bf16[144,1536]{1,0:T(8,128)(2,1)S(1)} collective-permute-done((bf16[144,1536]{1,0:T(8,128)(2,1)S(1)}, bf16[144,1536]{1,0:T(8,128)(2,1)S(1)}, u32[]{:S(2)}, u32[]{:S(2)}) %collective-permute-start.1) | collective-permute-done | bytes 442400 | tf_op jit(solution)/shard_map/ppermute | solution.py:16
  113.4 0.8 copy.17
  114.2 0.8 copy.18
  (6 shorter events, 0.0 us)
Async XLA Ops:
  7.2 54.5 %reduce-scatter.3.cloned.1.call-start = ((), (), s32[]{:S(2)}) async-start(), calls=%async_computation.2 | async-start | bytes 2211840 | tf_op jit(solution)/shard_map/reduce_scatter | solution.py:296
  7.9 1.5 %copy-start = (bf16[1,576,1536]{2,1,0:T(8,128)(2,1)S(1)}, bf16[1,576,1536]{2,1,0:T(8,128)(2,1)}, u32[]{:S(2)}) copy-start(bf16[1,576,1536]{2,1,0:T(8,128)(2,1)} %x_hbm.2) | copy-start | bytes 5308420
  9.4 1.7 %copy-start.1 = (bf16[2,1,1536,384]{3,2,1,0:T(8,128)(2,1)S(1)}, bf16[2,1,1536,384]{3,2,1,0:T(8,128)(2,1)}, u32[]{:S(2)}) copy-start(bf16[2,1,1536,384]{3,2,1,0:T(8,128)(2,1)} %wq_hbm.3) | copy-start | bytes 7077892
  11.1 0.7 copy-start.2
  21.9 1.5 %copy-start.3 = (bf16[1,576,1536]{2,1,0:T(8,128)(2,1)S(1)}, bf16[1,576,1536]{2,1,0:T(8,128)(2,1)}, u32[]{:S(2)}) copy-start(bf16[1,576,1536]{2,1,0:T(8,128)(2,1)} %x_hbm.3) | copy-start | bytes 5308420
  22.0 1.5 %copy-start.4 = (s32[1,8]{1,0:T(1,128)S(1)}, s32[1,8]{1,0:T(1,128)}, u32[]{:S(2)}) copy-start(s32[1,8]{1,0:T(1,128)} %lengths_ref.3) | copy-start | bytes 100
  22.0 79.7 %reduce-scatter.5.cloned.1.call-start = ((), (), s32[]{:S(2)}) async-start(), calls=%async_computation.3 | async-start | bytes 2211840 | tf_op jit(solution)/shard_map/reduce_scatter | solution.py:299
  40.5 64.3 %collective-permute-start.2 = (bf16[384,1536]{1,0:T(8,128)(2,1)S(1)}, bf16[384,1536]{1,0:T(8,128)(2,1)S(1)}, u32[]{:S(2)}, u32[]{:S(2)}) collective-permute-start(bf16[384,1536]{1,0:T(8,128)(2,1)S(1)} %get-tuple-element.6), channel_id=1, source_target_pairs={{0,28},{4,24},{8,20},{12,16},{16,12},{20,8},{24,4},{28,0},{1,29},{... | collective-permute-start | bytes 3538952 | tf_op jit(solution)/shard_map/ppermute | solution.py:21
  63.0 43.6 %collective-permute-start = (bf16[144,1536]{1,0:T(8,128)(2,1)S(1)}, bf16[144,1536]{1,0:T(8,128)(2,1)S(1)}, u32[]{:S(2)}, u32[]{:S(2)}) collective-permute-start(bf16[144,1536]{1,0:T(8,128)(2,1)S(1)} %fusion.1), channel_id=1, source_target_pairs={{0,4},{4,8},{8,12},{12,16},{16,20},{20,24},{24,28},{1,5},{5,9},{9,... | collective-permute-start | bytes 1327112 | tf_op jit(solution)/shard_map/ppermute | solution.py:16
  102.9 10.5 %collective-permute-start.1 = (bf16[144,1536]{1,0:T(8,128)(2,1)S(1)}, bf16[144,1536]{1,0:T(8,128)(2,1)S(1)}, u32[]{:S(2)}, u32[]{:S(2)}) collective-permute-start(bf16[144,1536]{1,0:T(8,128)(2,1)S(1)} %fusion), channel_id=1, source_target_pairs={{0,4},{4,8},{8,12},{12,16},{16,20},{20,24},{24,28},{1,5},{5,9},{9,... | collective-permute-start | bytes 1327112 | tf_op jit(solution)/shard_map/ppermute | solution.py:16
Sparse Core Ops, SparseCore 0:
  22.1 39.5 reduce-scatter.2
  64.1 37.4 reduce-scatter.4

commit v3 on v2

--- a/solution.py
+++ b/solution.py
@@ -14,6 +14,44 @@
     peers = lax.axis_size(axis)
     pairs = [(i, i + by) for i in range(peers) if 0 <= i + by < peers]
     return lax.ppermute(value, axis, pairs)
+
+
+def chain_sums_along(term, own_rows, axis, along):
+    peers = lax.axis_size(axis)
+    here = lax.axis_index(axis)
+    share = term.shape[0] // peers
+
+    def rows_of(owner):
+        owner = jnp.clip(owner, 0, peers - 1)
+        return lax.dynamic_slice_in_dim(term, owner * share, share, 0).astype(jnp.float32)
+
+    own = passed_along((own_rows.astype(jnp.float32) + rows_of(here)).astype(jnp.bfloat16), along, 1)
+    from_left = jnp.zeros((share, term.shape[1]), jnp.bfloat16)
+    from_right = from_left
+    for step in range(1, peers):
+        going_right = (rows_of(peers - step + here) + from_left.astype(jnp.float32)).astype(
+            jnp.bfloat16
+        )
+        going_left = (rows_of(here + step - peers) + from_right.astype(jnp.float32)).astype(
+            jnp.bfloat16
+        )
+        right = [(i, i + 1) for i in range(step)]
+        left = [(peers - 1 - i, peers - 2 - i) for i in range(step)]
+        names = axis
+        if step == peers - 1:
+            names = (along, axis)
+            right, left = (
+                [
+                    (stage * peers + source, (stage + 1) * peers + target)
+                    for stage in range(lax.axis_size(along) - 1)
+                    for source, target in pairs
+                ]
+                for pairs in (right, left)
+            )
+        from_left = lax.ppermute(going_right, names, right)
+        from_right = lax.ppermute(going_left, names, left)
+    total = own.astype(jnp.float32) + from_left.astype(jnp.float32)
+    return (total + from_right.astype(jnp.float32)).astype(jnp.bfloat16)
 
 
 def mirror_exchange(value, axis):
@@ -293,18 +331,10 @@
         value_weight,
         out_weight,
     )
-    summed_forward = lax.psum_scatter(
-        forward_term, "tensor", scatter_dimension=0, tiled=True
-    ).astype(jnp.float32)
-    summed_backward = lax.psum_scatter(
-        backward_term, "tensor", scatter_dimension=0, tiled=True
-    ).astype(jnp.float32)
     forward_rows = lax.dynamic_slice_in_dim(forward_in, row_start, share_rows, 0)
     cotangent_rows = lax.dynamic_slice_in_dim(cotangent, row_start, share_rows, 0)
-    section_rows = (forward_rows.astype(jnp.float32) + summed_forward).astype(jnp.bfloat16)
-    grad_rows = (cotangent_rows.astype(jnp.float32) + summed_backward).astype(jnp.bfloat16)
-    moved_section = passed_along(section_rows, "pipe", 1)
-    moved_grad = passed_along(grad_rows, "pipe", 1)
+    moved_section = chain_sums_along(forward_term, forward_rows, "tensor", "pipe")
+    moved_grad = chain_sums_along(backward_term, cotangent_rows, "tensor", "pipe")
     mirrored = mirror_exchange(weight_grad, "pipe").astype(jnp.float32)
     return (moved_section[None], moved_grad[None], mirrored[None])
 

time: 122 us -> 106 us (0.87)
  waiting for transfers between devices: 63.9 us -> 19.4 us
  starting transfers between devices: 5.03 us -> 42.7 us
  between operations: 14.1 us -> 0.84 us
  other arithmetic: 4.19 us -> 8.49 us
    reduce_scatter x2 -> x0, waiting for transfers between devices: 57 us -> none  [the longest x1 36.8 us: per_device(): lax.psum_scatter(backward_term, 'tensor', scatter_dimension=0, tiled=True)]
    ppermute x0 -> x12, starting transfers between devices: none -> 37.3 us  [the longest x6 30.5 us: chain_sums_along(): from_left = lax.ppermute(going_right, names, right)]
    ppermute x0 -> x12, waiting for transfers between devices: none -> 19.4 us  [the longest x6 12.5 us: chain_sums_along(): from_right = lax.ppermute(going_left, names, left)]
    ppermute x2, waiting for transfers between devices: 6.89 us -> 0.01 us  [passed_along(): return lax.ppermute(value, axis, pairs)]
    broadcast_in_dim x1 -> x3, other arithmetic: 1.7 us -> 4.82 us  [per_device(): return (moved_section[None], moved_grad[None], mirrored[None])]
    unnamed x13 -> x11, local copies, waits for them, and re-layouts: 7.23 us -> 4.51 us
    dynamic_slice x0 -> x2, local copies, waits for them, and re-layouts: none -> 1.96 us  [rows_of(): lax.dynamic_slice_in_dim(term, owner * share, share, 0).astype(jnp.float32)]
    convert_element_type x2 -> x4, other arithmetic: 2.5 us -> 3.67 us  [the longest x2 3.21 us: chain_sums_along(): (own_rows.astype(jnp.float32) + rows_of(here)).astype(jnp.bfloat16)]
  transfers between devices with their start and end apart: 5 -> 15, of which waited for: 3 -> 5; matrix products, arithmetic and copies ran while one was open for 3% -> 8% of each run, Pallas kernels for 14% -> 17%
where the time goes in v3:
time: 106 us; the launch traced here: 105 us
  starting transfers between devices  42.7 us (40%)
  Pallas kernels  26.7 us (25%)
  waiting for transfers between devices  19.4 us (18%)
  other arithmetic  8.49 us (8%)
  local copies, waits for them, and re-layouts  6.47 us (6%)
    ppermute x6, starting transfers between devices, chain_sums_along(): from_left = lax.ppermute(going_right, names, right)  30.5 us
    pallas_call x1, Pallas kernels, backward_terms_of(): pl.pallas_call(backward_kernel, out_shape=(jax.ShapeDtypeStruct((rows, wi...  17.7 us
    ppermute x6, waiting for transfers between devices, chain_sums_along(): from_right = lax.ppermute(going_left, names, left)  12.5 us
    pallas_call x1, Pallas kernels, forward_term_of(): pl.pallas_call(forward_kernel, out_shape=jax.ShapeDtypeStruct((rows, wide...  9.02 us
    ppermute x6, waiting for transfers between devices, chain_sums_along(): from_left = lax.ppermute(going_right, names, right)  6.84 us
    ppermute x6, starting transfers between devices, chain_sums_along(): from_right = lax.ppermute(going_left, names, left)  6.82 us
    broadcast_in_dim x3, other arithmetic, per_device(): return (moved_section[None], moved_grad[None], mirrored[None])  4.82 us
    ppermute x2, starting transfers between devices, passed_along(): return lax.ppermute(value, axis, pairs)  4.8 us
  transfers between devices with their start and end apart: 15, of which 5 were waited for; matrix products, arithmetic and copies ran while one was open for 8% of the time, Pallas kernels for 17%

profile of v3, /device:TPU:4, one launch (start us, length us, event | category | flops | bytes accessed | tf_op | source)
XLA Modules:
  0.0 104.6 jit_solution(10308891825981297672)
XLA Ops:
  1.4 1.5 %copy-done = bf16[1,576,1536]{2,1,0:T(8,128)(2,1)S(1)} copy-done((bf16[1,576,1536]{2,1,0:T(8,128)(2,1)S(1)}, bf16[1,576,1536]{2,1,0:T(8,128)(2,1)}, u32[]{:S(2)}) %copy-start) | copy-done | bytes 1769496
  2.8 1.7 %copy-done.1 = bf16[2,1,1536,384]{3,2,1,0:T(8,128)(2,1)S(1)} copy-done((bf16[2,1,1536,384]{3,2,1,0:T(8,128)(2,1)S(1)}, bf16[2,1,1536,384]{3,2,1,0:T(8,128)(2,1)}, u32[]{:S(2)}) %copy-start.1) | copy-done | bytes 2359320
  5.1 9.0 %forward_section.1 = bf16[576,1536]{1,0:T(8,128)(2,1)S(1)} custom-call(s32[1,8]{1,0:T(1,128)S(1)} %copy-done.2, bf16[2,1,1536]{2,1,0:T(2,128)(2,1)S(1)} %copy.13.gain_ref, bf16[1,576,1536]{2,1,0:T(8,128)(2,1)S(1)} %copy-done, bf16[2,1,1536,384]{3,2,1,0:T(8,128)(2,1)S(1)} %copy-done.1, bf16[2,1,1536,384]{3,2,1,0:T(8,128)(2,1)} %wk_hbm.3, ...), custom_call_target="tpu_custom_call" | custom-call | flops 2717908992 | bytes 11796480 | tf_op jit(solution)/shard_map/forward_section/pallas_call | solution.py:253
  15.2 4.2 %collective-permute-start.1 = (bf16[144,1536]{1,0:T(8,128)(2,1)}, bf16[144,1536]{1,0:T(8,128)(2,1)}, u32[]{:S(2)}, u32[]{:S(2)}) collective-permute-start(bf16[144,1536]{1,0:T(8,128)(2,1)} %get-tuple-element.19), channel_id=1, source_target_pairs={{0,1},{4,5},{8,9},{12,13},{16,17},{20,21},{24,25},{28,29}} | collective-permute-start | bytes 1327112 | tf_op jit(solution)/shard_map/ppermute | solution.py:51
  19.4 1.4 %collective-permute-start.4 = (bf16[144,1536]{1,0:T(8,128)(2,1)}, bf16[144,1536]{1,0:T(8,128)(2,1)}, u32[]{:S(2)}, u32[]{:S(2)}) collective-permute-start(bf16[144,1536]{1,0:T(8,128)(2,1)} %get-tuple-element.20), channel_id=1, source_target_pairs={{3,2},{7,6},{11,10},{15,14},{19,18},{23,22},{27,26},{31,30}} | collective-permute-start | bytes 1327112 | tf_op jit(solution)/shard_map/ppermute | solution.py:52
  20.9 17.7 %backward_section.1 = (bf16[576,1536]{1,0:T(8,128)(2,1)S(1)}, bf16[384,1536]{1,0:T(8,128)(2,1)}) custom-call(s32[1,8]{1,0:T(1,128)S(1)} %copy-done.4, bf16[2,1,1536]{2,1,0:T(2,128)(2,1)S(1)} %copy.13.gain_ref, bf16[1,576,1536]{2,1,0:T(8,128)(2,1)S(1)} %copy-done.3, bf16[1,576,1536]{2,1,0:T(8,128)(2,1)} %c_hbm.1, bf16[2,1,1536,384]{3,2,1,0:T(8,128)(2,1)} %wq_hbm.3, ...), custom_call_target="tpu_custom_call" | custom-call | flops 5435817984 | bytes 11796480 | tf_op jit(solution)/shard_map/backward_section/pallas_call | solution.py:277
  38.5 1.0 constant_dynamic-slice_fusion
  39.5 2.1 %collective-permute-start.8 = (bf16[144,1536]{1,0:T(8,128)(2,1)}, bf16[144,1536]{1,0:T(8,128)(2,1)}, u32[]{:S(2)}, u32[]{:S(2)}) collective-permute-start(bf16[144,1536]{1,0:T(8,128)(2,1)} %get-tuple-element.12), channel_id=1, source_target_pairs={{0,1},{4,5},{8,9},{12,13},{16,17},{20,21},{24,25},{28,29}} | collective-permute-start | bytes 1327112 | tf_op jit(solution)/shard_map/ppermute | solution.py:51
  41.6 1.4 %collective-permute-start.11 = (bf16[144,1536]{1,0:T(8,128)(2,1)}, bf16[144,1536]{1,0:T(8,128)(2,1)}, u32[]{:S(2)}, u32[]{:S(2)}) collective-permute-start(bf16[144,1536]{1,0:T(8,128)(2,1)} %get-tuple-element.13), channel_id=1, source_target_pairs={{3,2},{7,6},{11,10},{15,14},{19,18},{23,22},{27,26},{31,30}} | collective-permute-start | bytes 1327112 | tf_op jit(solution)/shard_map/ppermute | solution.py:52
  43.6 1.6 %fusion.1 = (bf16[144,1536]{1,0:T(8,128)(2,1)S(1)}, bf16[144,1536]{1,0:T(8,128)(2,1)S(1)}, bf16[144,1536]{1,0:T(8,128)(2,1)S(1)}) fusion(bf16[576,1536]{1,0:T(8,128)(2,1)S(1)} %forward_section.1, s32[]{:T(128)S(6)} %select_n.33, bf16[1,576,1536]{2,1,0:T(8,128)(2,1)} %x_hbm.2, s32[]{:T(128)S(6)} %select_n.32, bf16[144,1536]{1,0:T(8,128)(2,1)} %collective-permute-done.4, ...), kind=kLoop, calls=%fused_computation.4 | loop fusion | flops 2654208 | bytes 3981328 | tf_op jit(solution)/shard_map/convert_element_type | solution.py:28
  45.2 2.9 %collective-permute-start = (bf16[144,1536]{1,0:T(8,128)(2,1)S(1)}, bf16[144,1536]{1,0:T(8,128)(2,1)S(1)}, u32[]{:S(2)}, u32[]{:S(2)}) collective-permute-start(bf16[144,1536]{1,0:T(8,128)(2,1)S(1)} %get-tuple-element.14), channel_id=1, source_target_pairs={{0,4},{4,8},{8,12},{12,16},{16,20},{20,24},{24,28},{1,5},{5,9},{9,... | collective-permute-start | bytes 1327112 | tf_op jit(solution)/shard_map/ppermute | solution.py:16
  48.8 1.7 %collective-permute-done.8 = bf16[144,1536]{1,0:T(8,128)(2,1)} collective-permute-done((bf16[144,1536]{1,0:T(8,128)(2,1)}, bf16[144,1536]{1,0:T(8,128)(2,1)}, u32[]{:S(2)}, u32[]{:S(2)}) %collective-permute-start.8) | collective-permute-done | bytes 442400 | tf_op jit(solution)/shard_map/ppermute | solution.py:51
  50.5 4.4 %collective-permute-start.2 = (bf16[144,1536]{1,0:T(8,128)(2,1)S(1)}, bf16[144,1536]{1,0:T(8,128)(2,1)S(1)}, u32[]{:S(2)}, u32[]{:S(2)}) collective-permute-start(bf16[144,1536]{1,0:T(8,128)(2,1)S(1)} %get-tuple-element.16), channel_id=1, source_target_pairs={{0,1},{1,2},{4,5},{5,6},{8,9},{9,10},{12,13},{13,14},{16,17},{17,1... | collective-permute-start | bytes 1327112 | tf_op jit(solution)/shard_map/ppermute | solution.py:51
  55.0 1.6 %fusion = (bf16[144,1536]{1,0:T(8,128)(2,1)S(1)}, bf16[144,1536]{1,0:T(8,128)(2,1)S(1)}, bf16[144,1536]{1,0:T(8,128)(2,1)S(1)}) fusion(bf16[576,1536]{1,0:T(8,128)(2,1)S(1)} %get-tuple-element.5, s32[]{:T(128)S(6)} %select_n.33, bf16[1,576,1536]{2,1,0:T(8,128)(2,1)} %c_hbm.1, s32[]{:T(128)S(6)} %select_n.32, bf16[144,1536]{1,0:T(8,128)(2,1)} %collective-permute-done.11, ...), kind=kLoop, calls=%fused_computation.2 | loop fusion | flops 2654208 | bytes 3981328 | tf_op jit(solution)/shard_map/convert_element_type | solution.py:28
  56.6 1.9 %collective-permute-start.7 = (bf16[144,1536]{1,0:T(8,128)(2,1)S(1)}, bf16[144,1536]{1,0:T(8,128)(2,1)S(1)}, u32[]{:S(2)}, u32[]{:S(2)}) collective-permute-start(bf16[144,1536]{1,0:T(8,128)(2,1)S(1)} %get-tuple-element.7), channel_id=1, source_target_pairs={{0,4},{4,8},{8,12},{12,16},{16,20},{20,24},{24,28},{1,5},{5,9},{9,... | collective-permute-start | bytes 1327112 | tf_op jit(solution)/shard_map/ppermute | solution.py:16
  59.2 4.2 %collective-permute-done.2 = bf16[144,1536]{1,0:T(8,128)(2,1)S(1)} collective-permute-done((bf16[144,1536]{1,0:T(8,128)(2,1)S(1)}, bf16[144,1536]{1,0:T(8,128)(2,1)S(1)}, u32[]{:S(2)}, u32[]{:S(2)}) %collective-permute-start.2) | collective-permute-done | bytes 442400 | tf_op jit(solution)/shard_map/ppermute | solution.py:51
  63.5 4.4 %collective-permute-start.9 = (bf16[144,1536]{1,0:T(8,128)(2,1)S(1)}, bf16[144,1536]{1,0:T(8,128)(2,1)S(1)}, u32[]{:S(2)}, u32[]{:S(2)}) collective-permute-start(bf16[144,1536]{1,0:T(8,128)(2,1)S(1)} %get-tuple-element.9), channel_id=1, source_target_pairs={{0,1},{1,2},{4,5},{5,6},{8,9},{9,10},{12,13},{13,14},{16,17},{17,1... | collective-permute-start | bytes 1327112 | tf_op jit(solution)/shard_map/ppermute | solution.py:51
  68.1 8.6 %collective-permute-start.3 = (bf16[144,1536]{1,0:T(8,128)(2,1)S(1)}, bf16[144,1536]{1,0:T(8,128)(2,1)S(1)}, u32[]{:S(2)}, u32[]{:S(2)}) collective-permute-start(bf16[144,1536]{1,0:T(8,128)(2,1)S(1)} %get-tuple-element.17), channel_id=1, source_target_pairs={{0,5},{1,6},{2,7},{4,9},{5,10},{6,11},{8,13},{9,14},{10,15},{12,17... | collective-permute-start | bytes 1327112 | tf_op jit(solution)/shard_map/ppermute | solution.py:51
  76.7 1.3 %collective-permute-start.6 = (bf16[144,1536]{1,0:T(8,128)(2,1)S(1)}, bf16[144,1536]{1,0:T(8,128)(2,1)S(1)}, u32[]{:S(2)}, u32[]{:S(2)}) collective-permute-start(bf16[144,1536]{1,0:T(8,128)(2,1)S(1)} %get-tuple-element.18), channel_id=1, source_target_pairs={{3,6},{2,5},{1,4},{7,10},{6,9},{5,8},{11,14},{10,13},{9,12},{15,18... | collective-permute-start | bytes 1327112 | tf_op jit(solution)/shard_map/ppermute | solution.py:52
  78.2 6.8 %collective-permute-start.10 = (bf16[144,1536]{1,0:T(8,128)(2,1)S(1)}, bf16[144,1536]{1,0:T(8,128)(2,1)S(1)}, u32[]{:S(2)}, u32[]{:S(2)}) collective-permute-start(bf16[144,1536]{1,0:T(8,128)(2,1)S(1)} %get-tuple-element.10), channel_id=1, source_target_pairs={{0,5},{1,6},{2,7},{4,9},{5,10},{6,11},{8,13},{9,14},{10,15},{12,17... | collective-permute-start | bytes 1327112 | tf_op jit(solution)/shard_map/ppermute | solution.py:51
  85.1 3.0 %bitcast_convert_fusion = f32[1,384,1536]{2,1,0:T(8,128)} fusion(bf16[384,1536]{1,0:T(8,128)(2,1)} %collective-permute-done.14), kind=kLoop, calls=%fused_computation | loop fusion | flops 589824 | bytes 3538944 | tf_op jit(solution)/shard_map/broadcast_in_dim | solution.py:339
  88.1 1.3 %collective-permute-start.13 = (bf16[144,1536]{1,0:T(8,128)(2,1)S(1)}, bf16[144,1536]{1,0:T(8,128)(2,1)S(1)}, u32[]{:S(2)}, u32[]{:S(2)}) collective-permute-start(bf16[144,1536]{1,0:T(8,128)(2,1)S(1)} %get-tuple-element.11), channel_id=1, source_target_pairs={{3,6},{2,5},{1,4},{7,10},{6,9},{5,8},{11,14},{10,13},{9,12},{15,18... | collective-permute-start | bytes 1327112 | tf_op jit(solution)/shard_map/ppermute | solution.py:52
  89.4 4.6 %collective-permute-done.6 = bf16[144,1536]{1,0:T(8,128)(2,1)S(1)} collective-permute-done((bf16[144,1536]{1,0:T(8,128)(2,1)S(1)}, bf16[144,1536]{1,0:T(8,128)(2,1)S(1)}, u32[]{:S(2)}, u32[]{:S(2)}) %collective-permute-start.6) | collective-permute-done | bytes 442400 | tf_op jit(solution)/shard_map/ppermute | solution.py:52
  95.7 7.9 %collective-permute-done.13 = bf16[144,1536]{1,0:T(8,128)(2,1)S(1)} collective-permute-done((bf16[144,1536]{1,0:T(8,128)(2,1)S(1)}, bf16[144,1536]{1,0:T(8,128)(2,1)S(1)}, u32[]{:S(2)}, u32[]{:S(2)}) %collective-permute-start.13) | collective-permute-done | bytes 442400 | tf_op jit(solution)/shard_map/ppermute | solution.py:52
  (28 shorter events, 7.5 us)
Async XLA Ops:
  1.3 1.5 %copy-start = (bf16[1,576,1536]{2,1,0:T(8,128)(2,1)S(1)}, bf16[1,576,1536]{2,1,0:T(8,128)(2,1)}, u32[]{:S(2)}) copy-start(bf16[1,576,1536]{2,1,0:T(8,128)(2,1)} %x_hbm.2) | copy-start | bytes 5308420
  2.8 1.7 %copy-start.1 = (bf16[2,1,1536,384]{3,2,1,0:T(8,128)(2,1)S(1)}, bf16[2,1,1536,384]{3,2,1,0:T(8,128)(2,1)}, u32[]{:S(2)}) copy-start(bf16[2,1,1536,384]{3,2,1,0:T(8,128)(2,1)} %wq_hbm.3) | copy-start | bytes 7077892
  4.5 0.7 copy-start.2
  14.2 6.7 %copy-start.3 = (bf16[1,576,1536]{2,1,0:T(8,128)(2,1)S(1)}, bf16[1,576,1536]{2,1,0:T(8,128)(2,1)}, u32[]{:S(2)}) copy-start(bf16[1,576,1536]{2,1,0:T(8,128)(2,1)} %x_hbm.3) | copy-start | bytes 5308420
  14.2 6.7 %copy-start.4 = (s32[1,8]{1,0:T(1,128)S(1)}, s32[1,8]{1,0:T(1,128)}, u32[]{:S(2)}) copy-start(s32[1,8]{1,0:T(1,128)} %lengths_ref.3) | copy-start | bytes 100
  15.2 28.4 %collective-permute-start.1 = (bf16[144,1536]{1,0:T(8,128)(2,1)}, bf16[144,1536]{1,0:T(8,128)(2,1)}, u32[]{:S(2)}, u32[]{:S(2)}) collective-permute-start(bf16[144,1536]{1,0:T(8,128)(2,1)} %get-tuple-element.19), channel_id=1, source_target_pairs={{0,1},{4,5},{8,9},{12,13},{16,17},{20,21},{24,25},{28,29}} | collective-permute-start | bytes 1327112 | tf_op jit(solution)/shard_map/ppermute | solution.py:51
  19.4 24.2 %collective-permute-start.4 = (bf16[144,1536]{1,0:T(8,128)(2,1)}, bf16[144,1536]{1,0:T(8,128)(2,1)}, u32[]{:S(2)}, u32[]{:S(2)}) collective-permute-start(bf16[144,1536]{1,0:T(8,128)(2,1)} %get-tuple-element.20), channel_id=1, source_target_pairs={{3,2},{7,6},{11,10},{15,14},{19,18},{23,22},{27,26},{31,30}} | collective-permute-start | bytes 1327112 | tf_op jit(solution)/shard_map/ppermute | solution.py:52
  39.5 11.0 %collective-permute-start.8 = (bf16[144,1536]{1,0:T(8,128)(2,1)}, bf16[144,1536]{1,0:T(8,128)(2,1)}, u32[]{:S(2)}, u32[]{:S(2)}) collective-permute-start(bf16[144,1536]{1,0:T(8,128)(2,1)} %get-tuple-element.12), channel_id=1, source_target_pairs={{0,1},{4,5},{8,9},{12,13},{16,17},{20,21},{24,25},{28,29}} | collective-permute-start | bytes 1327112 | tf_op jit(solution)/shard_map/ppermute | solution.py:51
  41.6 13.4 %collective-permute-start.11 = (bf16[144,1536]{1,0:T(8,128)(2,1)}, bf16[144,1536]{1,0:T(8,128)(2,1)}, u32[]{:S(2)}, u32[]{:S(2)}) collective-permute-start(bf16[144,1536]{1,0:T(8,128)(2,1)} %get-tuple-element.13), channel_id=1, source_target_pairs={{3,2},{7,6},{11,10},{15,14},{19,18},{23,22},{27,26},{31,30}} | collective-permute-start | bytes 1327112 | tf_op jit(solution)/shard_map/ppermute | solution.py:52
  43.0 35.2 %collective-permute-start.14 = (bf16[384,1536]{1,0:T(8,128)(2,1)}, bf16[384,1536]{1,0:T(8,128)(2,1)}, u32[]{:S(2)}, u32[]{:S(2)}) collective-permute-start(bf16[384,1536]{1,0:T(8,128)(2,1)} %get-tuple-element.6), channel_id=1, source_target_pairs={{0,28},{4,24},{8,20},{12,16},{16,12},{20,8},{24,4},{28,0},{1,29},{... | collective-permute-start | bytes 3538952 | tf_op jit(solution)/shard_map/ppermute | solution.py:59
  45.2 42.8 %collective-permute-start = (bf16[144,1536]{1,0:T(8,128)(2,1)S(1)}, bf16[144,1536]{1,0:T(8,128)(2,1)S(1)}, u32[]{:S(2)}, u32[]{:S(2)}) collective-permute-start(bf16[144,1536]{1,0:T(8,128)(2,1)S(1)} %get-tuple-element.14), channel_id=1, source_target_pairs={{0,4},{4,8},{8,12},{12,16},{16,20},{20,24},{24,28},{1,5},{5,9},{9,... | collective-permute-start | bytes 1327112 | tf_op jit(solution)/shard_map/ppermute | solution.py:16
  48.1 10.4 %collective-permute-start.5 = (bf16[144,1536]{1,0:T(8,128)(2,1)S(1)}, bf16[144,1536]{1,0:T(8,128)(2,1)S(1)}, u32[]{:S(2)}, u32[]{:S(2)}) collective-permute-start(bf16[144,1536]{1,0:T(8,128)(2,1)S(1)} %get-tuple-element.15), channel_id=1, source_target_pairs={{3,2},{2,1},{7,6},{6,5},{11,10},{10,9},{15,14},{14,13},{19,18},{18... | collective-permute-start | bytes 1327112 | tf_op jit(solution)/shard_map/ppermute | solution.py:52
  50.5 12.9 %collective-permute-start.2 = (bf16[144,1536]{1,0:T(8,128)(2,1)S(1)}, bf16[144,1536]{1,0:T(8,128)(2,1)S(1)}, u32[]{:S(2)}, u32[]{:S(2)}) collective-permute-start(bf16[144,1536]{1,0:T(8,128)(2,1)S(1)} %get-tuple-element.16), channel_id=1, source_target_pairs={{0,1},{1,2},{4,5},{5,6},{8,9},{9,10},{12,13},{13,14},{16,17},{17,1... | collective-permute-start | bytes 1327112 | tf_op jit(solution)/shard_map/ppermute | solution.py:51
  56.6 38.3 %collective-permute-start.7 = (bf16[144,1536]{1,0:T(8,128)(2,1)S(1)}, bf16[144,1536]{1,0:T(8,128)(2,1)S(1)}, u32[]{:S(2)}, u32[]{:S(2)}) collective-permute-start(bf16[144,1536]{1,0:T(8,128)(2,1)S(1)} %get-tuple-element.7), channel_id=1, source_target_pairs={{0,4},{4,8},{8,12},{12,16},{16,20},{20,24},{24,28},{1,5},{5,9},{9,... | collective-permute-start | bytes 1327112 | tf_op jit(solution)/shard_map/ppermute | solution.py:16
  58.5 9.6 %collective-permute-start.12 = (bf16[144,1536]{1,0:T(8,128)(2,1)S(1)}, bf16[144,1536]{1,0:T(8,128)(2,1)S(1)}, u32[]{:S(2)}, u32[]{:S(2)}) collective-permute-start(bf16[144,1536]{1,0:T(8,128)(2,1)S(1)} %get-tuple-element.8), channel_id=1, source_target_pairs={{3,2},{2,1},{7,6},{6,5},{11,10},{10,9},{15,14},{14,13},{19,18},{18... | collective-permute-start | bytes 1327112 | tf_op jit(solution)/shard_map/ppermute | solution.py:52
  63.5 13.2 %collective-permute-start.9 = (bf16[144,1536]{1,0:T(8,128)(2,1)S(1)}, bf16[144,1536]{1,0:T(8,128)(2,1)S(1)}, u32[]{:S(2)}, u32[]{:S(2)}) collective-permute-start(bf16[144,1536]{1,0:T(8,128)(2,1)S(1)} %get-tuple-element.9), channel_id=1, source_target_pairs={{0,1},{1,2},{4,5},{5,6},{8,9},{9,10},{12,13},{13,14},{16,17},{17,1... | collective-permute-start | bytes 1327112 | tf_op jit(solution)/shard_map/ppermute | solution.py:51
  68.1 21.2 %collective-permute-start.3 = (bf16[144,1536]{1,0:T(8,128)(2,1)S(1)}, bf16[144,1536]{1,0:T(8,128)(2,1)S(1)}, u32[]{:S(2)}, u32[]{:S(2)}) collective-permute-start(bf16[144,1536]{1,0:T(8,128)(2,1)S(1)} %get-tuple-element.17), channel_id=1, source_target_pairs={{0,5},{1,6},{2,7},{4,9},{5,10},{6,11},{8,13},{9,14},{10,15},{12,17... | collective-permute-start | bytes 1327112 | tf_op jit(solution)/shard_map/ppermute | solution.py:51
  76.7 17.3 %collective-permute-start.6 = (bf16[144,1536]{1,0:T(8,128)(2,1)S(1)}, bf16[144,1536]{1,0:T(8,128)(2,1)S(1)}, u32[]{:S(2)}, u32[]{:S(2)}) collective-permute-start(bf16[144,1536]{1,0:T(8,128)(2,1)S(1)} %get-tuple-element.18), channel_id=1, source_target_pairs={{3,6},{2,5},{1,4},{7,10},{6,9},{5,8},{11,14},{10,13},{9,12},{15,18... | collective-permute-start | bytes 1327112 | tf_op jit(solution)/shard_map/ppermute | solution.py:52
  78.2 17.5 %collective-permute-start.10 = (bf16[144,1536]{1,0:T(8,128)(2,1)S(1)}, bf16[144,1536]{1,0:T(8,128)(2,1)S(1)}, u32[]{:S(2)}, u32[]{:S(2)}) collective-permute-start(bf16[144,1536]{1,0:T(8,128)(2,1)S(1)} %get-tuple-element.10), channel_id=1, source_target_pairs={{0,5},{1,6},{2,7},{4,9},{5,10},{6,11},{8,13},{9,14},{10,15},{12,17... | collective-permute-start | bytes 1327112 | tf_op jit(solution)/shard_map/ppermute | solution.py:51
  88.1 15.6 %collective-permute-start.13 = (bf16[144,1536]{1,0:T(8,128)(2,1)S(1)}, bf16[144,1536]{1,0:T(8,128)(2,1)S(1)}, u32[]{:S(2)}, u32[]{:S(2)}) collective-permute-start(bf16[144,1536]{1,0:T(8,128)(2,1)S(1)} %get-tuple-element.11), channel_id=1, source_target_pairs={{3,6},{2,5},{1,4},{7,10},{6,9},{5,8},{11,14},{10,13},{9,12},{15,18... | collective-permute-start | bytes 1327112 | tf_op jit(solution)/shard_map/ppermute | solution.py:52

commit v4 on v3

--- a/solution.py
+++ b/solution.py
@@ -163,8 +163,8 @@
 
 
 def backward_kernel(
-    lengths_ref, gain_ref, x_hbm, c_hbm, wq_hbm, wk_hbm, wv_hbm, wo_hbm, out_ref, grad_ref,
-    x_ref, c_ref, w_ref, wo_ref, qkv_ref, dqkv_ref, att_ref, sems,
+    lengths_ref, gain_ref, x_hbm, c_hbm, wq_hbm, wk_hbm, wv_hbm, wo_hbm, out_ref, att_ref,
+    x_ref, c_ref, w_ref, wo_ref, qkv_ref, dqkv_ref, sems,
 ):
     width = wq_hbm.shape[3]
     copies = start_copies(
@@ -235,11 +235,6 @@
         scale = scales[block]
         pull = jnp.mean(d_normed * widened, axis=-1, keepdims=True) * scale * scale * scale
         out_ref[low:high, :] = (d_normed * scale - widened * pull).astype(jnp.bfloat16)
-    for head in range(heads):
-        at = head * HEAD_DIM
-        grad_ref[at : at + HEAD_DIM, :] = dot_tn(
-            att_ref[:, at : at + HEAD_DIM], c_ref[...]
-        ).astype(jnp.bfloat16)
 
 
 SMEM_SPEC = pl.BlockSpec(memory_space=pltpu.SMEM)
@@ -278,7 +273,7 @@
         backward_kernel,
         out_shape=(
             jax.ShapeDtypeStruct((rows, wide), bf16),
-            jax.ShapeDtypeStruct((width, wide), bf16),
+            jax.ShapeDtypeStruct((rows, width), bf16),
         ),
         in_specs=[SMEM_SPEC, VMEM_SPEC] + [ANY_SPEC] * 6,
         out_specs=(VMEM_SPEC, VMEM_SPEC),
@@ -289,7 +284,6 @@
             pltpu.VMEM((width, wide), bf16),
             pltpu.VMEM((rows, 3 * width), bf16),
             pltpu.VMEM((rows, 3 * width), bf16),
-            pltpu.VMEM((rows, width), bf16),
             pltpu.SemaphoreType.DMA((6,)),
         ],
         compiler_params=pltpu.CompilerParams(vmem_limit_bytes=VMEM_LIMIT),
@@ -321,7 +315,7 @@
     forward_term = forward_term_of(
         fwd_lengths, norm_gains, fwd_inputs, query_weight, key_weight, value_weight, out_weight
     )
-    backward_term, weight_grad = backward_terms_of(
+    backward_term, attended = backward_terms_of(
         bwd_lengths,
         norm_gains,
         bwd_inputs,
@@ -331,6 +325,7 @@
         value_weight,
         out_weight,
     )
+    weight_grad = dot_tn(attended, cotangent).astype(jnp.bfloat16)
     forward_rows = lax.dynamic_slice_in_dim(forward_in, row_start, share_rows, 0)
     cotangent_rows = lax.dynamic_slice_in_dim(cotangent, row_start, share_rows, 0)
     moved_section = chain_sums_along(forward_term, forward_rows, "tensor", "pipe")

time: 106 us -> 99.7 us (0.941)
  starting transfers between devices: 42.7 us -> 34.6 us
  matrix products: 0 us -> 2.13 us
  Pallas kernels: 26.7 us -> 24.7 us
  waiting for transfers between devices: 19.4 us -> 20.8 us
    ppermute x6, starting transfers between devices: 30.5 us -> 21.8 us  [chain_sums_along(): from_left = lax.ppermute(going_right, names, right)]
    ppermute x6, waiting for transfers between devices: 6.84 us -> 9.77 us  [chain_sums_along(): from_left = lax.ppermute(going_right, names, right)]
    dot_general x0 -> x1, matrix products: none -> 2.13 us  [dot_tn(): lax.dot_general(left, right, (((0,), (0,)), ((), ())), preferred_element_...]
    pallas_call x1, Pallas kernels: 17.7 us -> 15.7 us  [backward_terms_of(): pl.pallas_call(backward_kernel, out_shape=(jax.ShapeDtypeStruct((rows, wi...]
    ppermute x6, waiting for transfers between devices: 12.5 us -> 11 us  [chain_sums_along(): from_right = lax.ppermute(going_left, names, left)]
    unnamed x11 -> x15, local copies, waits for them, and re-layouts: 4.51 us -> 4.33 us
  transfers between devices with their start and end apart: 15 -> 15, of which waited for: 5 -> 6; matrix products, arithmetic and copies ran while one was open for 8% -> 11% of each run, Pallas kernels for 17% -> 9%
where the time goes in v4:
time: 99.7 us; the launch traced here: 97.8 us
  starting transfers between devices  34.6 us (35%)
  Pallas kernels  24.7 us (25%)
  waiting for transfers between devices  20.8 us (21%)
  other arithmetic  8.49 us (9%)
  local copies, waits for them, and re-layouts  6.29 us (6%)
  matrix products  2.13 us (2%)
    ppermute x6, starting transfers between devices, chain_sums_along(): from_left = lax.ppermute(going_right, names, right)  21.8 us
    pallas_call x1, Pallas kernels, backward_terms_of(): pl.pallas_call(backward_kernel, out_shape=(jax.ShapeDtypeStruct((rows, wi...  15.7 us
    ppermute x6, waiting for transfers between devices, chain_sums_along(): from_right = lax.ppermute(going_left, names, left)  11 us
    ppermute x6, waiting for transfers between devices, chain_sums_along(): from_left = lax.ppermute(going_right, names, right)  9.77 us
    pallas_call x1, Pallas kernels, forward_term_of(): pl.pallas_call(forward_kernel, out_shape=jax.ShapeDtypeStruct((rows, wide...  9.01 us
    ppermute x6, starting transfers between devices, chain_sums_along(): from_right = lax.ppermute(going_left, names, left)  6.83 us
    ppermute x2, starting transfers between devices, passed_along(): return lax.ppermute(value, axis, pairs)  5.38 us
    broadcast_in_dim x3, other arithmetic, per_device(): return (moved_section[None], moved_grad[None], mirrored[None])  4.82 us
  transfers between devices with their start and end apart: 15, of which 6 were waited for; matrix products, arithmetic and copies ran while one was open for 11% of the time, Pallas kernels for 9%

profile of v4, /device:TPU:4, one launch (start us, length us, event | category | flops | bytes accessed | tf_op | source)
XLA Modules:
  0.0 97.8 jit_solution(16754673863538920873)
XLA Ops:
  1.4 1.5 %copy-done.2 = bf16[1,576,1536]{2,1,0:T(8,128)(2,1)S(1)} copy-done((bf16[1,576,1536]{2,1,0:T(8,128)(2,1)S(1)}, bf16[1,576,1536]{2,1,0:T(8,128)(2,1)}, u32[]{:S(2)}) %copy-start.2) | copy-done | bytes 1769496
  2.8 1.5 %copy-done.5 = bf16[1,576,1536]{2,1,0:T(8,128)(2,1)S(1)} copy-done((bf16[1,576,1536]{2,1,0:T(8,128)(2,1)S(1)}, bf16[1,576,1536]{2,1,0:T(8,128)(2,1)}, u32[]{:S(2)}) %copy-start.5) | copy-done | bytes 1769496
  5.0 15.7 %backward_section.1 = (bf16[576,1536]{1,0:T(8,128)(2,1)S(1)}, bf16[576,384]{1,0:T(8,128)(2,1)S(1)}) custom-call(s32[1,8]{1,0:T(1,128)S(1)} %copy-done.6, bf16[2,1,1536]{2,1,0:T(2,128)(2,1)S(1)} %copy.13.gain_ref, bf16[1,576,1536]{2,1,0:T(8,128)(2,1)S(1)} %copy-done.5, bf16[1,576,1536]{2,1,0:T(8,128)(2,1)S(1)} %copy-done.2, bf16[2,1,1536,384]{3,2,1,0:T(8,128)(2,1)} %wq_hbm.3, ...), custom_call_target="tpu_custom_call" | custom-call | flops 5435817984 | bytes 11796480 | tf_op jit(solution)/shard_map/backward_section/pallas_call | solution.py:272
  21.7 1.5 %collective-permute-start.11 = (bf16[144,1536]{1,0:T(8,128)(2,1)}, bf16[144,1536]{1,0:T(8,128)(2,1)}, u32[]{:S(2)}, u32[]{:S(2)}) collective-permute-start(bf16[144,1536]{1,0:T(8,128)(2,1)} %get-tuple-element.13), channel_id=1, source_target_pairs={{3,2},{7,6},{11,10},{15,14},{19,18},{23,22},{27,26},{31,30}} | collective-permute-start | bytes 1327112 | tf_op jit(solution)/shard_map/ppermute | solution.py:52
  23.2 4.2 %collective-permute-start.8 = (bf16[144,1536]{1,0:T(8,128)(2,1)}, bf16[144,1536]{1,0:T(8,128)(2,1)}, u32[]{:S(2)}, u32[]{:S(2)}) collective-permute-start(bf16[144,1536]{1,0:T(8,128)(2,1)} %get-tuple-element.12), channel_id=1, source_target_pairs={{0,1},{4,5},{8,9},{12,13},{16,17},{20,21},{24,25},{28,29}} | collective-permute-start | bytes 1327112 | tf_op jit(solution)/shard_map/ppermute | solution.py:51
  27.4 9.0 %forward_section.1 = bf16[576,1536]{1,0:T(8,128)(2,1)S(1)} custom-call(s32[1,8]{1,0:T(1,128)S(1)} %copy-done.4, bf16[2,1,1536]{2,1,0:T(2,128)(2,1)S(1)} %copy.13.gain_ref, bf16[1,576,1536]{2,1,0:T(8,128)(2,1)S(1)} %copy-done, bf16[2,1,1536,384]{3,2,1,0:T(8,128)(2,1)S(1)} %copy-done.1, bf16[2,1,1536,384]{3,2,1,0:T(8,128)(2,1)} %wk_hbm.3, ...), custom_call_target="tpu_custom_call" | custom-call | flops 2717908992 | bytes 11796480 | tf_op jit(solution)/shard_map/forward_section/pallas_call | solution.py:248
  37.4 2.1 %collective-permute-start.1 = (bf16[144,1536]{1,0:T(8,128)(2,1)}, bf16[144,1536]{1,0:T(8,128)(2,1)}, u32[]{:S(2)}, u32[]{:S(2)}) collective-permute-start(bf16[144,1536]{1,0:T(8,128)(2,1)} %get-tuple-element.19), channel_id=1, source_target_pairs={{0,1},{4,5},{8,9},{12,13},{16,17},{20,21},{24,25},{28,29}} | collective-permute-start | bytes 1327112 | tf_op jit(solution)/shard_map/ppermute | solution.py:51
  39.5 1.4 %collective-permute-start.4 = (bf16[144,1536]{1,0:T(8,128)(2,1)}, bf16[144,1536]{1,0:T(8,128)(2,1)}, u32[]{:S(2)}, u32[]{:S(2)}) collective-permute-start(bf16[144,1536]{1,0:T(8,128)(2,1)} %get-tuple-element.20), channel_id=1, source_target_pairs={{3,2},{7,6},{11,10},{15,14},{19,18},{23,22},{27,26},{31,30}} | collective-permute-start | bytes 1327112 | tf_op jit(solution)/shard_map/ppermute | solution.py:52
  40.9 2.1 %convolution_convert_fusion = bf16[384,1536]{1,0:T(8,128)(2,1)} fusion(bf16[576,384]{1,0:T(8,128)(2,1)S(1)} %get-tuple-element.6, bf16[1,576,1536]{2,1,0:T(8,128)(2,1)S(1)} %copy-done.3), kind=kOutput, calls=%fused_computation | convolution fusion | flops 680067072 | bytes 3391488 | tf_op jit(solution)/shard_map/dot_general | solution.py:83
  43.6 1.6 %fusion.1 = (bf16[144,1536]{1,0:T(8,128)(2,1)S(1)}, bf16[144,1536]{1,0:T(8,128)(2,1)S(1)}, bf16[144,1536]{1,0:T(8,128)(2,1)S(1)}) fusion(bf16[576,1536]{1,0:T(8,128)(2,1)S(1)} %get-tuple-element.5, s32[]{:T(128)S(6)} %select_n.33, bf16[1,576,1536]{2,1,0:T(8,128)(2,1)} %c_hbm.1, s32[]{:T(128)S(6)} %select_n.32, bf16[144,1536]{1,0:T(8,128)(2,1)} %collective-permute-done.11, ...), kind=kLoop, calls=%fused_computation.4 | loop fusion | flops 2654208 | bytes 3981328 | tf_op jit(solution)/shard_map/convert_element_type | solution.py:28
  45.9 1.3 %collective-permute-start.9 = (bf16[144,1536]{1,0:T(8,128)(2,1)S(1)}, bf16[144,1536]{1,0:T(8,128)(2,1)S(1)}, u32[]{:S(2)}, u32[]{:S(2)}) collective-permute-start(bf16[144,1536]{1,0:T(8,128)(2,1)S(1)} %get-tuple-element.9), channel_id=1, source_target_pairs={{0,1},{1,2},{4,5},{5,6},{8,9},{9,10},{12,13},{13,14},{16,17},{17,1... | collective-permute-start | bytes 1327112 | tf_op jit(solution)/shard_map/ppermute | solution.py:51
  48.4 1.9 %collective-permute-start.7 = (bf16[144,1536]{1,0:T(8,128)(2,1)S(1)}, bf16[144,1536]{1,0:T(8,128)(2,1)S(1)}, u32[]{:S(2)}, u32[]{:S(2)}) collective-permute-start(bf16[144,1536]{1,0:T(8,128)(2,1)S(1)} %get-tuple-element.7), channel_id=1, source_target_pairs={{0,4},{4,8},{8,12},{12,16},{16,20},{20,24},{24,28},{1,5},{5,9},{9,... | collective-permute-start | bytes 1327112 | tf_op jit(solution)/shard_map/ppermute | solution.py:16
  50.3 1.6 %fusion.2 = (bf16[144,1536]{1,0:T(8,128)(2,1)S(1)}, bf16[144,1536]{1,0:T(8,128)(2,1)S(1)}, bf16[144,1536]{1,0:T(8,128)(2,1)S(1)}) fusion(bf16[576,1536]{1,0:T(8,128)(2,1)S(1)} %forward_section.1, s32[]{:T(128)S(6)} %select_n.33, bf16[1,576,1536]{2,1,0:T(8,128)(2,1)} %x_hbm.2, s32[]{:T(128)S(6)} %select_n.32, bf16[144,1536]{1,0:T(8,128)(2,1)} %collective-permute-done.4, ...), kind=kLoop, calls=%fused_computation.6 | loop fusion | flops 2654208 | bytes 3981328 | tf_op jit(solution)/shard_map/convert_element_type | solution.py:28
  52.0 4.4 %collective-permute-start.2 = (bf16[144,1536]{1,0:T(8,128)(2,1)S(1)}, bf16[144,1536]{1,0:T(8,128)(2,1)S(1)}, u32[]{:S(2)}, u32[]{:S(2)}) collective-permute-start(bf16[144,1536]{1,0:T(8,128)(2,1)S(1)} %get-tuple-element.16), channel_id=1, source_target_pairs={{0,1},{1,2},{4,5},{5,6},{8,9},{9,10},{12,13},{13,14},{16,17},{17,1... | collective-permute-start | bytes 1327112 | tf_op jit(solution)/shard_map/ppermute | solution.py:51
  57.5 3.5 %collective-permute-start = (bf16[144,1536]{1,0:T(8,128)(2,1)S(1)}, bf16[144,1536]{1,0:T(8,128)(2,1)S(1)}, u32[]{:S(2)}, u32[]{:S(2)}) collective-permute-start(bf16[144,1536]{1,0:T(8,128)(2,1)S(1)} %get-tuple-element.14), channel_id=1, source_target_pairs={{0,4},{4,8},{8,12},{12,16},{16,20},{20,24},{24,28},{1,5},{5,9},{9,... | collective-permute-start | bytes 1327112 | tf_op jit(solution)/shard_map/ppermute | solution.py:16
  61.2 5.1 %collective-permute-done.2 = bf16[144,1536]{1,0:T(8,128)(2,1)S(1)} collective-permute-done((bf16[144,1536]{1,0:T(8,128)(2,1)S(1)}, bf16[144,1536]{1,0:T(8,128)(2,1)S(1)}, u32[]{:S(2)}, u32[]{:S(2)}) %collective-permute-start.2) | collective-permute-done | bytes 442400 | tf_op jit(solution)/shard_map/ppermute | solution.py:51
  66.3 5.2 %collective-permute-start.10 = (bf16[144,1536]{1,0:T(8,128)(2,1)S(1)}, bf16[144,1536]{1,0:T(8,128)(2,1)S(1)}, u32[]{:S(2)}, u32[]{:S(2)}) collective-permute-start(bf16[144,1536]{1,0:T(8,128)(2,1)S(1)} %get-tuple-element.10), channel_id=1, source_target_pairs={{0,5},{1,6},{2,7},{4,9},{5,10},{6,11},{8,13},{9,14},{10,15},{12,17... | collective-permute-start | bytes 1327112 | tf_op jit(solution)/shard_map/ppermute | solution.py:51
  71.5 1.3 %collective-permute-start.13 = (bf16[144,1536]{1,0:T(8,128)(2,1)S(1)}, bf16[144,1536]{1,0:T(8,128)(2,1)S(1)}, u32[]{:S(2)}, u32[]{:S(2)}) collective-permute-start(bf16[144,1536]{1,0:T(8,128)(2,1)S(1)} %get-tuple-element.11), channel_id=1, source_target_pairs={{3,6},{2,5},{1,4},{7,10},{6,9},{5,8},{11,14},{10,13},{9,12},{15,18... | collective-permute-start | bytes 1327112 | tf_op jit(solution)/shard_map/ppermute | solution.py:52
  73.1 4.6 %collective-permute-start.3 = (bf16[144,1536]{1,0:T(8,128)(2,1)S(1)}, bf16[144,1536]{1,0:T(8,128)(2,1)S(1)}, u32[]{:S(2)}, u32[]{:S(2)}) collective-permute-start(bf16[144,1536]{1,0:T(8,128)(2,1)S(1)} %get-tuple-element.17), channel_id=1, source_target_pairs={{0,5},{1,6},{2,7},{4,9},{5,10},{6,11},{8,13},{9,14},{10,15},{12,17... | collective-permute-start | bytes 1327112 | tf_op jit(solution)/shard_map/ppermute | solution.py:51
  77.6 3.0 %bitcast_convert_fusion = f32[1,384,1536]{2,1,0:T(8,128)} fusion(bf16[384,1536]{1,0:T(8,128)(2,1)} %collective-permute-done.14), kind=kLoop, calls=%fused_computation.2 | loop fusion | flops 589824 | bytes 3538944 | tf_op jit(solution)/shard_map/broadcast_in_dim | solution.py:334
  80.6 1.3 %collective-permute-start.6 = (bf16[144,1536]{1,0:T(8,128)(2,1)S(1)}, bf16[144,1536]{1,0:T(8,128)(2,1)S(1)}, u32[]{:S(2)}, u32[]{:S(2)}) collective-permute-start(bf16[144,1536]{1,0:T(8,128)(2,1)S(1)} %get-tuple-element.18), channel_id=1, source_target_pairs={{3,6},{2,5},{1,4},{7,10},{6,9},{5,8},{11,14},{10,13},{9,12},{15,18... | collective-permute-start | bytes 1327112 | tf_op jit(solution)/shard_map/ppermute | solution.py:52
  81.9 5.1 %collective-permute-done.13 = bf16[144,1536]{1,0:T(8,128)(2,1)S(1)} collective-permute-done((bf16[144,1536]{1,0:T(8,128)(2,1)S(1)}, bf16[144,1536]{1,0:T(8,128)(2,1)S(1)}, u32[]{:S(2)}, u32[]{:S(2)}) %collective-permute-start.13) | collective-permute-done | bytes 442400 | tf_op jit(solution)/shard_map/ppermute | solution.py:52
  88.0 3.1 %collective-permute-done.3 = bf16[144,1536]{1,0:T(8,128)(2,1)S(1)} collective-permute-done((bf16[144,1536]{1,0:T(8,128)(2,1)S(1)}, bf16[144,1536]{1,0:T(8,128)(2,1)S(1)}, u32[]{:S(2)}, u32[]{:S(2)}) %collective-permute-start.3) | collective-permute-done | bytes 442400 | tf_op jit(solution)/shard_map/ppermute | solution.py:51
  91.1 5.9 %collective-permute-done.6 = bf16[144,1536]{1,0:T(8,128)(2,1)S(1)} collective-permute-done((bf16[144,1536]{1,0:T(8,128)(2,1)S(1)}, bf16[144,1536]{1,0:T(8,128)(2,1)S(1)}, u32[]{:S(2)}, u32[]{:S(2)}) %collective-permute-start.6) | collective-permute-done | bytes 442400 | tf_op jit(solution)/shard_map/ppermute | solution.py:52
  (33 shorter events, 9.2 us)
Async XLA Ops:
  1.3 1.5 %copy-start.2 = (bf16[1,576,1536]{2,1,0:T(8,128)(2,1)S(1)}, bf16[1,576,1536]{2,1,0:T(8,128)(2,1)}, u32[]{:S(2)}) copy-start(bf16[1,576,1536]{2,1,0:T(8,128)(2,1)} %c_hbm.1) | copy-start | bytes 5308420
  2.8 1.5 %copy-start.5 = (bf16[1,576,1536]{2,1,0:T(8,128)(2,1)S(1)}, bf16[1,576,1536]{2,1,0:T(8,128)(2,1)}, u32[]{:S(2)}) copy-start(bf16[1,576,1536]{2,1,0:T(8,128)(2,1)} %x_hbm.3) | copy-start | bytes 5308420
  4.3 0.7 copy-start.6
  5.0 22.4 %copy-start.1 = (bf16[2,1,1536,384]{3,2,1,0:T(8,128)(2,1)S(1)}, bf16[2,1,1536,384]{3,2,1,0:T(8,128)(2,1)}, u32[]{:S(2)}) copy-start(bf16[2,1,1536,384]{3,2,1,0:T(8,128)(2,1)} %wq_hbm.3) | copy-start | bytes 7077892
  20.7 6.7 %copy-start = (bf16[1,576,1536]{2,1,0:T(8,128)(2,1)S(1)}, bf16[1,576,1536]{2,1,0:T(8,128)(2,1)}, u32[]{:S(2)}) copy-start(bf16[1,576,1536]{2,1,0:T(8,128)(2,1)} %x_hbm.2) | copy-start | bytes 5308420
  20.7 6.7 %copy-start.4 = (s32[1,8]{1,0:T(1,128)S(1)}, s32[1,8]{1,0:T(1,128)}, u32[]{:S(2)}) copy-start(s32[1,8]{1,0:T(1,128)} %lengths_ref.2) | copy-start | bytes 100
  21.7 21.9 %collective-permute-start.11 = (bf16[144,1536]{1,0:T(8,128)(2,1)}, bf16[144,1536]{1,0:T(8,128)(2,1)}, u32[]{:S(2)}, u32[]{:S(2)}) collective-permute-start(bf16[144,1536]{1,0:T(8,128)(2,1)} %get-tuple-element.13), channel_id=1, source_target_pairs={{3,2},{7,6},{11,10},{15,14},{19,18},{23,22},{27,26},{31,30}} | collective-permute-start | bytes 1327112 | tf_op jit(solution)/shard_map/ppermute | solution.py:52
  23.2 20.5 %collective-permute-start.8 = (bf16[144,1536]{1,0:T(8,128)(2,1)}, bf16[144,1536]{1,0:T(8,128)(2,1)}, u32[]{:S(2)}, u32[]{:S(2)}) collective-permute-start(bf16[144,1536]{1,0:T(8,128)(2,1)} %get-tuple-element.12), channel_id=1, source_target_pairs={{0,1},{4,5},{8,9},{12,13},{16,17},{20,21},{24,25},{28,29}} | collective-permute-start | bytes 1327112 | tf_op jit(solution)/shard_map/ppermute | solution.py:51
  36.4 4.5 %copy-start.3 = (bf16[1,576,1536]{2,1,0:T(8,128)(2,1)S(1)}, bf16[1,576,1536]{2,1,0:T(8,128)(2,1)}, u32[]{:S(2)}) copy-start(bf16[1,576,1536]{2,1,0:T(8,128)(2,1)} %c_hbm.1) | copy-start | bytes 5308420
  37.4 11.0 %collective-permute-start.1 = (bf16[144,1536]{1,0:T(8,128)(2,1)}, bf16[144,1536]{1,0:T(8,128)(2,1)}, u32[]{:S(2)}, u32[]{:S(2)}) collective-permute-start(bf16[144,1536]{1,0:T(8,128)(2,1)} %get-tuple-element.19), channel_id=1, source_target_pairs={{0,1},{4,5},{8,9},{12,13},{16,17},{20,21},{24,25},{28,29}} | collective-permute-start | bytes 1327112 | tf_op jit(solution)/shard_map/ppermute | solution.py:51
  39.5 10.9 %collective-permute-start.4 = (bf16[144,1536]{1,0:T(8,128)(2,1)}, bf16[144,1536]{1,0:T(8,128)(2,1)}, u32[]{:S(2)}, u32[]{:S(2)}) collective-permute-start(bf16[144,1536]{1,0:T(8,128)(2,1)} %get-tuple-element.20), channel_id=1, source_target_pairs={{3,2},{7,6},{11,10},{15,14},{19,18},{23,22},{27,26},{31,30}} | collective-permute-start | bytes 1327112 | tf_op jit(solution)/shard_map/ppermute | solution.py:52
  43.0 30.0 %collective-permute-start.14 = (bf16[384,1536]{1,0:T(8,128)(2,1)}, bf16[384,1536]{1,0:T(8,128)(2,1)}, u32[]{:S(2)}, u32[]{:S(2)}) collective-permute-start(bf16[384,1536]{1,0:T(8,128)(2,1)} %convolution_convert_fusion), channel_id=1, source_target_pairs={{0,28},{4,24},{8,20},{12,16},{16,12},{20,8},{24,4},{28,0},{1,29},{... | collective-permute-start | bytes 3538952 | tf_op jit(solution)/shard_map/ppermute | solution.py:59
  45.2 11.2 %collective-permute-start.12 = (bf16[144,1536]{1,0:T(8,128)(2,1)S(1)}, bf16[144,1536]{1,0:T(8,128)(2,1)S(1)}, u32[]{:S(2)}, u32[]{:S(2)}) collective-permute-start(bf16[144,1536]{1,0:T(8,128)(2,1)S(1)} %get-tuple-element.8), channel_id=1, source_target_pairs={{3,2},{2,1},{7,6},{6,5},{11,10},{10,9},{15,14},{14,13},{19,18},{18... | collective-permute-start | bytes 1327112 | tf_op jit(solution)/shard_map/ppermute | solution.py:52
  45.9 11.6 %collective-permute-start.9 = (bf16[144,1536]{1,0:T(8,128)(2,1)S(1)}, bf16[144,1536]{1,0:T(8,128)(2,1)S(1)}, u32[]{:S(2)}, u32[]{:S(2)}) collective-permute-start(bf16[144,1536]{1,0:T(8,128)(2,1)S(1)} %get-tuple-element.9), channel_id=1, source_target_pairs={{0,1},{1,2},{4,5},{5,6},{8,9},{9,10},{12,13},{13,14},{16,17},{17,1... | collective-permute-start | bytes 1327112 | tf_op jit(solution)/shard_map/ppermute | solution.py:51
  48.4 32.2 %collective-permute-start.7 = (bf16[144,1536]{1,0:T(8,128)(2,1)S(1)}, bf16[144,1536]{1,0:T(8,128)(2,1)S(1)}, u32[]{:S(2)}, u32[]{:S(2)}) collective-permute-start(bf16[144,1536]{1,0:T(8,128)(2,1)S(1)} %get-tuple-element.7), channel_id=1, source_target_pairs={{0,4},{4,8},{8,12},{12,16},{16,20},{20,24},{24,28},{1,5},{5,9},{9,... | collective-permute-start | bytes 1327112 | tf_op jit(solution)/shard_map/ppermute | solution.py:16
  52.0 14.4 %collective-permute-start.2 = (bf16[144,1536]{1,0:T(8,128)(2,1)S(1)}, bf16[144,1536]{1,0:T(8,128)(2,1)S(1)}, u32[]{:S(2)}, u32[]{:S(2)}) collective-permute-start(bf16[144,1536]{1,0:T(8,128)(2,1)S(1)} %get-tuple-element.16), channel_id=1, source_target_pairs={{0,1},{1,2},{4,5},{5,6},{8,9},{9,10},{12,13},{13,14},{16,17},{17,1... | collective-permute-start | bytes 1327112 | tf_op jit(solution)/shard_map/ppermute | solution.py:51
  56.4 15.1 %collective-permute-start.5 = (bf16[144,1536]{1,0:T(8,128)(2,1)S(1)}, bf16[144,1536]{1,0:T(8,128)(2,1)S(1)}, u32[]{:S(2)}, u32[]{:S(2)}) collective-permute-start(bf16[144,1536]{1,0:T(8,128)(2,1)S(1)} %get-tuple-element.15), channel_id=1, source_target_pairs={{3,2},{2,1},{7,6},{6,5},{11,10},{10,9},{15,14},{14,13},{19,18},{18... | collective-permute-start | bytes 1327112 | tf_op jit(solution)/shard_map/ppermute | solution.py:52
  57.5 30.5 %collective-permute-start = (bf16[144,1536]{1,0:T(8,128)(2,1)S(1)}, bf16[144,1536]{1,0:T(8,128)(2,1)S(1)}, u32[]{:S(2)}, u32[]{:S(2)}) collective-permute-start(bf16[144,1536]{1,0:T(8,128)(2,1)S(1)} %get-tuple-element.14), channel_id=1, source_target_pairs={{0,4},{4,8},{8,12},{12,16},{16,20},{20,24},{24,28},{1,5},{5,9},{9,... | collective-permute-start | bytes 1327112 | tf_op jit(solution)/shard_map/ppermute | solution.py:16
  66.3 15.6 %collective-permute-start.10 = (bf16[144,1536]{1,0:T(8,128)(2,1)S(1)}, bf16[144,1536]{1,0:T(8,128)(2,1)S(1)}, u32[]{:S(2)}, u32[]{:S(2)}) collective-permute-start(bf16[144,1536]{1,0:T(8,128)(2,1)S(1)} %get-tuple-element.10), channel_id=1, source_target_pairs={{0,5},{1,6},{2,7},{4,9},{5,10},{6,11},{8,13},{9,14},{10,15},{12,17... | collective-permute-start | bytes 1327112 | tf_op jit(solution)/shard_map/ppermute | solution.py:51
  71.5 15.5 %collective-permute-start.13 = (bf16[144,1536]{1,0:T(8,128)(2,1)S(1)}, bf16[144,1536]{1,0:T(8,128)(2,1)S(1)}, u32[]{:S(2)}, u32[]{:S(2)}) collective-permute-start(bf16[144,1536]{1,0:T(8,128)(2,1)S(1)} %get-tuple-element.11), channel_id=1, source_target_pairs={{3,6},{2,5},{1,4},{7,10},{6,9},{5,8},{11,14},{10,13},{9,12},{15,18... | collective-permute-start | bytes 1327112 | tf_op jit(solution)/shard_map/ppermute | solution.py:52
  73.1 18.0 %collective-permute-start.3 = (bf16[144,1536]{1,0:T(8,128)(2,1)S(1)}, bf16[144,1536]{1,0:T(8,128)(2,1)S(1)}, u32[]{:S(2)}, u32[]{:S(2)}) collective-permute-start(bf16[144,1536]{1,0:T(8,128)(2,1)S(1)} %get-tuple-element.17), channel_id=1, source_target_pairs={{0,5},{1,6},{2,7},{4,9},{5,10},{6,11},{8,13},{9,14},{10,15},{12,17... | collective-permute-start | bytes 1327112 | tf_op jit(solution)/shard_map/ppermute | solution.py:51
  80.6 16.3 %collective-permute-start.6 = (bf16[144,1536]{1,0:T(8,128)(2,1)S(1)}, bf16[144,1536]{1,0:T(8,128)(2,1)S(1)}, u32[]{:S(2)}, u32[]{:S(2)}) collective-permute-start(bf16[144,1536]{1,0:T(8,128)(2,1)S(1)} %get-tuple-element.18), channel_id=1, source_target_pairs={{3,6},{2,5},{1,4},{7,10},{6,9},{5,8},{11,14},{10,13},{9,12},{15,18... | collective-permute-start | bytes 1327112 | tf_op jit(solution)/shard_map/ppermute | solution.py:52
